TPU v7x, 512 devices: a whole 4x8x8 slice. The times are simulated.
512 devices in a mesh: leaf: 128 (over y, z, core), rhs: 4 (over x).
Axes of the slice: x: 4, y: 8, z: 8, core: 2. Of those that a mesh axis runs over, the one named last changes fastest.
Arguments:
- obs_coef: float32 [128, 32768], P('rhs', 'leaf'), may hold values from -0.75 to 0.75
- obs_data: float32 [320, 32768], P('rhs', 'leaf'), may hold values from -6 to 6
- obs_target: int32 [32768], P('leaf'), may hold values from 0 to 511, as said below
- leaf_map: int32 [512], replicated, may hold values from 0 to 511, as said below
- leaf_parent: int32 [512], replicated, may hold values from 0 to 7
- leaf_inv: float32 [512, 128, 128], P('leaf'), may hold values from -0.5 to 1.5
- leaf_off: float32 [512, 128, 128], P('leaf'), may hold values from -0.0625 to 0.0625
- top_inv: float32 [8, 128, 128], replicated, may hold values from -0.5 to 1.5
- top_rhs: float32 [8, 320, 128], P(None, 'rhs'), may hold values from -6 to 6
Outputs:
- leaf_solution: float32 [512, 320, 128], P('leaf', 'rhs')
- top_solution: float32 [8, 320, 128], P(None, 'rhs')
Inputs may be any that keep to these rules, and one draw needn't show every extreme that they name: A permutation: supernode i is stored at position leaf_map[i], which lies on index leaf_map[i] // 4 of leaf. `obs_target`: the rows held by one index of leaf name supernodes stored on any one index of leaf at most 4 times; in every draw one index of leaf is named exactly 4 times by the rows of every index.
All inputs are finite; a program needn't handle non-finite values.
Results may differ from a plain program's by a relative error of at most 0.0003.
Values sent between devices are 32-bit elements; how exact they have to be, the bound alone decides.
No kernel may reach another device: no remote copies, remote signals or barrier semaphores. Data moves between devices by JAX's collectives and lax.ppermute only.
A program may use at most 64 MiB of HBM per device.

v0:
```python
import jax
import jax.numpy as jnp
from jax import lax
from jax.sharding import PartitionSpec as P


def body(
    obs_coef, obs_data, obs_target, leaf_map, leaf_parent, leaf_inv, leaf_off, top_inv, top_rhs
):
    highest = lax.Precision.HIGHEST
    groups = lax.axis_size("leaf")
    device_index = lax.axis_index("leaf")
    local_count = leaf_inv.shape[0]
    block_width = leaf_inv.shape[1]
    top_count = top_inv.shape[0]
    date_cols = obs_data.shape[0]
    rows_here = obs_target.shape[0]
    leaf_total = leaf_map.shape[0]
    capacity = max(2, 2 * rows_here // groups)
    slots_total = groups * capacity
    all_ids = jnp.arange(leaf_total, dtype=jnp.int32)
    id_match = obs_target[:, None] == all_ids[None, :]
    position = jnp.sum(jnp.where(id_match, leaf_map[None, :], 0), axis=1)
    owner_dev = position // local_count
    member = position % local_count
    row_ids = jnp.arange(rows_here, dtype=jnp.int32)
    earlier = (owner_dev[:, None] == owner_dev[None, :]) & (row_ids[:, None] > row_ids[None, :])
    queue_rank = jnp.sum(earlier.astype(jnp.int32), axis=1)
    target_slot = owner_dev * capacity + queue_rank
    slot_mark = (member + 1).astype(jnp.float32)[None, :]

    def place_rows(values):
        return jnp.zeros((values.shape[0], slots_total), jnp.float32).at[:, target_slot].set(values)

    coef_full = lax.all_gather(obs_coef, "rhs", axis=0, tiled=True)
    recv_coef, recv_data, recv_mark = (
        lax.all_to_all(place_rows(coef_full), "leaf", split_axis=1, concat_axis=1, tiled=True),
        lax.all_to_all(place_rows(obs_data), "leaf", split_axis=1, concat_axis=1, tiled=True),
        lax.all_to_all(place_rows(slot_mark), "leaf", split_axis=1, concat_axis=1, tiled=True),
    )
    slot_values = (jnp.arange(local_count, dtype=jnp.int32) + 1).astype(jnp.float32)
    chosen = (recv_mark[0][None, :] == slot_values[:, None]).astype(jnp.float32)
    spread = (recv_data[None, :, :] * chosen[:, None, :]).reshape(
        local_count * date_cols, slots_total
    )
    leaf_rhs = lax.dot_general(
        spread, recv_coef, (((1,), (1,)), ((), ())), precision=highest
    ).reshape(local_count, date_cols, block_width)
    solved = jnp.einsum("ltc,ldc->ltd", leaf_rhs, leaf_inv, precision=highest)
    update = jnp.einsum("ltd,lcd->ltc", solved, leaf_off, precision=highest)
    positions_here = device_index * local_count + jnp.arange(local_count, dtype=jnp.int32)
    holder_match = leaf_map[None, :] == positions_here[:, None]
    parent_here = jnp.sum(jnp.where(holder_match, leaf_parent[None, :], 0), axis=1)
    to_top = (parent_here[:, None] == jnp.arange(top_count, dtype=jnp.int32)[None, :]).astype(
        jnp.float32
    )
    contrib = jnp.einsum("lp,ltc->ptc", to_top, update, precision=highest)
    flat_terms = contrib.reshape(top_count * date_cols, block_width)
    top_total = lax.psum(flat_terms, "leaf").reshape(top_count, date_cols, block_width)
    residue = top_rhs - top_total
    top_solved = jnp.einsum("ptc,pdc->ptd", residue, top_inv, precision=highest)
    top_solution = jnp.einsum("ptd,pdc->ptc", top_solved, top_inv, precision=highest)
    from_top = jnp.einsum("lp,ptc->ltc", to_top, top_solution, precision=highest)
    lifted = jnp.einsum("ltc,lcd->ltd", from_top, leaf_off, precision=highest)
    leaf_solution = jnp.einsum("ltc,lcd->ltd", solved - lifted, leaf_inv, precision=highest)
    return (leaf_solution, top_solution)


def solution(mesh):
    return jax.shard_map(
        body,
        mesh=mesh,
        in_specs=(
            P("rhs", "leaf"),
            P("rhs", "leaf"),
            P("leaf"),
            P(),
            P(),
            P("leaf", None, None),
            P("leaf", None, None),
            P(),
            P(None, "rhs", None),
        ),
        out_specs=(P("leaf", "rhs", None), P(None, "rhs", None)),
        check_vma=False,
    )
```

profile of v0, /device:TPU:1, one launch (start us, length us, event | category | flops | bytes accessed | tf_op | source)
XLA Modules:
  0.0 287.3 jit_solution(1507953007622240396)
XLA Ops:
  7.2 0.0 copy-start
  7.2 0.9 select_reduce_fusion
  8.2 0.2 convert_reduce_fusion
  8.4 1.4 scatter_custom_fusion.1
  9.8 0.7 all_to_all.22
  10.5 0.0 copy-start.5
  10.5 18.5 %all-to-all-start.1 = ((f32[1,128,4]{2,0,1:T(1,128)}), f32[1,128,4]{2,0,1:T(1,128)S(1)}, u32[]{:S(2)}, u32[]{:S(2)}) async-start(f32[1,128,4]{2,0,1:T(1,128)} %bitcast.8), calls=%async_computation.1 | async-start | bytes 131072 | tf_op jit(solution)/shard_map/all_to_all | solution.py:39
  29.1 0.0 copy-done.5
  29.1 0.1 copy.37
  29.2 1.8 scatter_custom_fusion
  31.0 9.6 %all-to-all-done.1 = f32[1,128,4]{2,0,1:T(1,128)S(1)} async-done(((f32[1,128,4]{2,0,1:T(1,128)}), f32[1,128,4]{2,0,1:T(1,128)S(1)}, u32[]{:S(2)}, u32[]{:S(2)}) %all-to-all-start.1) | async-done | bytes 2080 | tf_op jit(solution)/shard_map/all_to_all | solution.py:39
  40.6 0.0 copy-start.6
  40.6 5.8 %all-to-all-start = ((f32[80,128,4]{0,2,1:T(4,128)}), f32[80,128,4]{0,2,1:T(4,128)S(1)}, u32[]{:S(2)}, u32[]{:S(2)}) async-start(f32[80,128,4]{0,2,1:T(4,128)} %bitcast.4), calls=%async_computation | async-start | bytes 524288 | tf_op jit(solution)/shard_map/all_to_all | solution.py:38
  46.4 0.0 copy-done.6
  46.4 10.3 %all_gather.3 = f32[128,256]{1,0:T(8,128)S(1)} all-gather(f32[32,256]{1,0:T(8,128)S(1)} %copy-done.6), channel_id=1, replica_groups=mesh['leaf'=128,'rhs'=4] {'rhs'}, dimensions={0}, use_global_device_ids=true | all-gather | bytes 163840 | tf_op jit(solution)/shard_map/all_gather | solution.py:35
  56.8 0.1 copy.40
  56.9 1.8 scatter_custom_fusion.2
  58.7 2.1 all-to-all-done
  60.7 0.0 copy-start.8
  60.7 13.9 %all-to-all-start.2 = ((f32[128,128,4]{0,2,1:T(4,128)}), f32[128,128,4]{0,2,1:T(4,128)S(1)}, u32[]{:S(2)}, u32[]{:S(2)}) async-start(f32[128,128,4]{0,2,1:T(4,128)} %bitcast.10), calls=%async_computation.2 | async-start | bytes 524288 | tf_op jit(solution)/shard_map/all_to_all | solution.py:37
  74.7 0.0 copy-start.7
  74.7 0.2 all-reduce.2.cloned.1.call-start
  74.9 0.0 copy-done.8
  74.9 0.4 copy-done.7
  75.4 0.2 select_reduce_fusion.1
  75.5 0.5 broadcast.224
  76.1 0.8 reduce.3
  76.9 0.1 eq.79
  77.0 0.1 compare_convert_fusion
  77.0 0.1 copy.38
  77.2 11.7 %all-to-all-done.2 = f32[128,128,4]{0,2,1:T(4,128)S(1)} async-done(((f32[128,128,4]{0,2,1:T(4,128)}), f32[128,128,4]{0,2,1:T(4,128)S(1)}, u32[]{:S(2)}, u32[]{:S(2)}) %all-to-all-start.2) | async-done | bytes 262176 | tf_op jit(solution)/shard_map/all_to_all | solution.py:37
  88.9 0.0 copy-start.3
  88.9 0.7 fusion
  89.6 0.3 copy-done.3
  89.8 0.0 copy-start.2
  89.8 0.6 fusion.26
  90.5 0.3 copy-done.2
  90.8 0.6 fusion.27
  91.4 0.0 copy-start.4
  91.4 1.1 fusion.10
  92.6 0.0 all-reduce.2.cloned.1.call-update
  92.6 183.2 %all-reduce.2.cloned.1.call-done = f32[8,80,128]{2,0,1:T(8,128)} async-done(((f32[8,80,128]{2,0,1:T(8,128)}), f32[8,80,128]{2,0,1:T(8,128)}) %all-reduce.2.cloned.1.call-update) | async-done | bytes 327696 | tf_op jit(solution)/shard_map/psum | solution.py:59
  275.8 0.0 copy-done.4
  275.8 1.1 copy_subtract_fusion
  276.9 0.0 copy-done
  276.9 1.1 fusion.4
  278.0 0.6 fusion.28
  278.6 0.0 copy-start.1
  278.6 0.4 fusion.2
  279.0 0.4 convolution_subtract_fusion
  279.4 0.0 copy-done.1
  279.4 1.0 fusion.29
  (5 shorter events, 0.0 us)
Async XLA Ops:
  7.2 269.7 %copy-start = (f32[8,128,128]{2,1,0:T(8,128)S(1)}, f32[8,128,128]{2,1,0:T(8,128)}, u32[]{:S(2)}) copy-start(f32[8,128,128]{2,1,0:T(8,128)} %param.16) | copy-start | bytes 1572868
  10.5 18.6 %copy-start.5 = (f32[80,256]{1,0:T(8,128)S(1)}, f32[80,256]{1,0:T(8,128)}, u32[]{:S(2)}) copy-start(f32[80,256]{1,0:T(8,128)} %param.10) | copy-start | bytes 245764
  10.5 30.1 %all-to-all-start.1 = ((f32[1,128,4]{2,0,1:T(1,128)}), f32[1,128,4]{2,0,1:T(1,128)S(1)}, u32[]{:S(2)}, u32[]{:S(2)}) async-start(f32[1,128,4]{2,0,1:T(1,128)} %bitcast.8), calls=%async_computation.1 | async-start | bytes 131072 | tf_op jit(solution)/shard_map/all_to_all | solution.py:39
  40.6 5.9 %copy-start.6 = (f32[32,256]{1,0:T(8,128)S(1)}, f32[32,256]{1,0:T(8,128)}, u32[]{:S(2)}) copy-start(f32[32,256]{1,0:T(8,128)} %param.9) | copy-start | bytes 98308
  40.6 20.2 %all-to-all-start = ((f32[80,128,4]{0,2,1:T(4,128)}), f32[80,128,4]{0,2,1:T(4,128)S(1)}, u32[]{:S(2)}, u32[]{:S(2)}) async-start(f32[80,128,4]{0,2,1:T(4,128)} %bitcast.4), calls=%async_computation | async-start | bytes 524288 | tf_op jit(solution)/shard_map/all_to_all | solution.py:38
  60.7 14.2 %copy-start.8 = (s32[512]{0:T(512)S(1)}, s32[512]{0:T(512)}, u32[]{:S(2)}) copy-start(s32[512]{0:T(512)} %param.13) | copy-start | bytes 6148
  60.7 28.2 %all-to-all-start.2 = ((f32[128,128,4]{0,2,1:T(4,128)}), f32[128,128,4]{0,2,1:T(4,128)S(1)}, u32[]{:S(2)}, u32[]{:S(2)}) async-start(f32[128,128,4]{0,2,1:T(4,128)} %bitcast.10), calls=%async_computation.2 | async-start | bytes 524288 | tf_op jit(solution)/shard_map/all_to_all | solution.py:37
  74.7 0.7 copy-start.7
  74.7 201.1 %all-reduce.2.cloned.1.call-start = ((), (), s32[]{:S(2)}) async-start(), calls=%async_computation.3 | async-start | bytes 655360 | tf_op jit(solution)/shard_map/psum | solution.py:59
  88.9 1.0 copy-start.3
  89.8 0.9 copy-start.2
  91.4 184.4 %copy-start.4 = (f32[8,80,128]{2,1,0:T(8,128)S(1)}, f32[8,80,128]{2,1,0:T(8,128)}, u32[]{:S(2)}) copy-start(f32[8,80,128]{2,1,0:T(8,128)} %param.17) | copy-start | bytes 983044
  278.6 0.8 copy-start.1
Sparse Core Ops, SparseCore 0:
  92.7 183.0 all-reduce.1
where the time goes:
time: 288 us; the launch traced here: 287 us
  waiting for transfers between devices  207 us (72%)
  starting transfers between devices  38.5 us (13%)
  between operations  14.3 us (5%)
  blocking collectives  10.3 us (4%)
  local copies, waits for them, and re-layouts  7.72 us (3%)
  matrix products  6.57 us (2%)
  other arithmetic  3.32 us (1%)
    psum x1, waiting for transfers between devices, body(): lax.psum(flat_terms, 'leaf').reshape(top_count, date_cols, block_width)  183 us
    all_to_all x1, starting transfers between devices, body(): lax.all_to_all(place_rows(slot_mark), 'leaf', split_axis=1, concat_axis=1...  18.5 us
    all_to_all x1, starting transfers between devices, body(): lax.all_to_all(place_rows(coef_full), 'leaf', split_axis=1, concat_axis=1...  13.9 us
    all_to_all x1, waiting for transfers between devices, body(): lax.all_to_all(place_rows(coef_full), 'leaf', split_axis=1, concat_axis=1...  11.7 us
    all_gather x1, blocking collectives, body(): coef_full = lax.all_gather(obs_coef, 'rhs', axis=0, tiled=True)  10.3 us
    all_to_all x1, waiting for transfers between devices, body(): lax.all_to_all(place_rows(slot_mark), 'leaf', split_axis=1, concat_axis=1...  9.59 us
    all_to_all x1, starting transfers between devices, body(): lax.all_to_all(place_rows(obs_data), 'leaf', split_axis=1, concat_axis=1,...  5.84 us
  transfers between devices with their start and end apart: 4, of which 4 were waited for; matrix products, arithmetic and copies ran while one was open for 2% of the time, Pallas kernels for 0%

commit v1 on v0

v1 whole, which is shorter than its diff:
```python
import jax
import jax.numpy as jnp
from jax import lax
from jax.sharding import Mesh, PartitionSpec as P

HI = lax.Precision.HIGHEST


def body(
    obs_coef, obs_data, obs_target, leaf_map, leaf_parent, leaf_inv, leaf_off, top_inv, top_rhs
):
    chips = lax.axis_size("chip")
    cores = lax.axis_size("core")
    q = lax.axis_index("chip")
    c = lax.axis_index("core")
    local = leaf_inv.shape[0]
    width = leaf_inv.shape[1]
    tops = top_inv.shape[0]
    dates = obs_data.shape[0]
    rows = obs_target.shape[0]
    shard = obs_coef.shape[0]
    total = leaf_map.shape[0]
    cap = 4
    slots = cores * cap
    half = tops // cores
    pieces = tops * dates // (chips * cores)
    span = dates // pieces

    ids = jnp.arange(total, dtype=jnp.int32)
    pos = jnp.sum(jnp.where(obs_target[:, None] == ids[None, :], leaf_map[None, :], 0), axis=1)
    owner = pos // local
    member = pos % local
    r = jnp.arange(rows, dtype=jnp.int32)
    earlier = (owner[:, None] == owner[None, :]) & (r[:, None] > r[None, :])
    rank = jnp.sum(earlier.astype(jnp.int32), axis=1)
    code = ((owner % cores) * chips + owner // cores) * slots + c * cap + rank
    meta = jnp.stack([(member + 1).astype(jnp.float32), code.astype(jnp.float32)])
    pad = jnp.zeros((6, rows), jnp.float32)
    payload = jnp.concatenate([obs_data, obs_coef, meta, pad], axis=0)
    pair = lax.all_gather(payload, "core", axis=0, tiled=False)
    codes = pair[:, dates + shard + 1, :]
    slot_ids = (c * chips * slots + jnp.arange(chips * slots, dtype=jnp.int32)).astype(jnp.float32)
    onehot = (slot_ids[:, None, None] == codes[None, :, :]).astype(jnp.float32)
    placed = lax.dot_general(onehot, pair, (((1, 2), (0, 2)), ((), ())), precision=HI)
    placed = jnp.pad(placed, ((0, 0), (0, 128 - placed.shape[1]))).reshape(chips, slots, 128)
    recv = lax.all_to_all(placed, "chip", 0, 0).reshape(chips * slots, 128)
    coef_t = lax.all_gather(recv[:, dates : dates + shard].T, "rhs", axis=0, tiled=True)
    data_t = recv[:, :dates].T
    mark = recv[:, dates + shard]
    want = (jnp.arange(local, dtype=jnp.int32) + 1).astype(jnp.float32)
    chosen = (mark[None, :] == want[:, None]).astype(jnp.float32)
    spread = (data_t[None] * chosen[:, None, :]).reshape(local * dates, chips * slots)
    rhs = lax.dot_general(spread, coef_t, (((1,), (1,)), ((), ())), precision=HI)
    rhs = rhs.reshape(local, dates, width)
    comb = jnp.einsum("lcd,lde->lce", leaf_off, leaf_inv, precision=HI)
    update = jnp.einsum("lte,lce->ltc", rhs, comb, precision=HI)
    both = lax.all_gather(update, "core", axis=0, tiled=True)

    solved = jnp.einsum("ltc,ldc->ltd", rhs, leaf_inv, precision=HI)
    base = jnp.einsum("ltc,lcd->ltd", solved, leaf_inv, precision=HI)

    first = q * cores * local
    places = first + jnp.arange(cores * local, dtype=jnp.int32)
    held = leaf_map[None, :] == places[:, None]
    parent = jnp.sum(jnp.where(held, leaf_parent[None, :], 0), axis=1)
    mine = c * half + jnp.arange(half, dtype=jnp.int32)
    to_top = (parent[None, :] == mine[:, None]).astype(jnp.float32)
    contrib = jnp.sum(to_top[:, :, None, None] * both[None], axis=1)
    parts = contrib.reshape(half, pieces, span, width).transpose(0, 2, 1, 3)
    parts = parts.reshape(chips, pieces * width)
    got = lax.all_to_all(parts, "chip", 0, 0)
    piece = jnp.sum(got, axis=0).reshape(pieces, width)

    p = c * half + q // span
    tt = q % span
    gram = jnp.einsum("pdc,pde->pce", top_inv, top_inv, precision=HI)
    gram_p = lax.dynamic_index_in_dim(gram, p, 0, keepdims=False)
    own_rhs = lax.dynamic_slice(
        top_rhs.reshape(tops, pieces, span, width), (p, 0, tt, 0), (1, pieces, 1, width)
    ).reshape(pieces, width)
    sol = lax.dot_general(own_rhs - piece, gram_p, (((1,), (0,)), ((), ())), precision=HI)
    out = jnp.broadcast_to(sol.reshape(1, pieces * width), (chips, pieces * width))
    full = lax.all_to_all(out, "chip", 0, 0)
    full = lax.all_gather(full, "core", axis=0, tiled=True)
    top_solution = full.reshape(tops, span, pieces, width).transpose(0, 2, 1, 3)
    top_solution = top_solution.reshape(tops, dates, width)

    my_parent = lax.dynamic_slice_in_dim(parent, c * local, local, 0)
    pick = (my_parent[:, None] == jnp.arange(tops, dtype=jnp.int32)[None, :]).astype(jnp.float32)
    from_top = jnp.sum(pick[:, :, None, None] * top_solution[None], axis=1)
    leaf_solution = base - jnp.einsum("ltc,lcd->ltd", from_top, comb, precision=HI)
    return (leaf_solution, top_solution)


def solution(mesh):
    devices = mesh.devices
    split = Mesh(devices.reshape(devices.shape[0] // 2, 2, -1), ("chip", "core", "rhs"))
    leaf = ("chip", "core")
    return jax.shard_map(
        body,
        mesh=split,
        in_specs=(
            P("rhs", leaf),
            P("rhs", leaf),
            P(leaf),
            P(),
            P(),
            P(leaf, None, None),
            P(leaf, None, None),
            P(),
            P(None, "rhs", None),
        ),
        out_specs=(P(leaf, "rhs", None), P(None, "rhs", None)),
        check_vma=False,
    )
```

time: 288 us -> 100 us (0.35)
  waiting for transfers between devices: 207 us -> 33.8 us
  blocking collectives: 10.3 us -> 30.9 us
  starting transfers between devices: 38.5 us -> 20.2 us
  between operations: 14.3 us -> 0.9 us
    psum x1 -> x0, waiting for transfers between devices: 183 us -> none  [body(): lax.psum(flat_terms, 'leaf').reshape(top_count, date_cols, block_width)]
    all_gather x1 -> x4, blocking collectives: 10.3 us -> 30.9 us  [the longest x1 9.72 us: body(): lax.all_gather(recv[:, dates:dates + shard].T, 'rhs', axis=0, tiled=True)]
    all_to_all x3, starting transfers between devices: 38.3 us -> 20.2 us  [the longest x1 11 us: body(): recv = lax.all_to_all(placed, 'chip', 0, 0).reshape(chips * slots, 128)]
    all_to_all x3, waiting for transfers between devices: 23.4 us -> 33.8 us  [the longest x1 12.3 us: body(): recv = lax.all_to_all(placed, 'chip', 0, 0).reshape(chips * slots, 128)]
    scatter x3 -> x0, local copies, waits for them, and re-layouts: 5.03 us -> none  [place_rows(): jnp.zeros((values.shape[0], slots_total), jnp.float32).at[:, target_slot]]
  transfers between devices with their start and end apart: 4 -> 3, of which waited for: 4 -> 3; matrix products, arithmetic and copies ran while one was open for 2% -> 3% of each run, Pallas kernels for 0% -> 0%
where the time goes in v1:
time: 100 us; the launch traced here: 99.8 us
  waiting for transfers between devices  33.8 us (34%)
  blocking collectives  30.9 us (31%)
  starting transfers between devices  20.2 us (20%)
  matrix products  5.52 us (6%)
  local copies, waits for them, and re-layouts  4.93 us (5%)
  other arithmetic  3.51 us (4%)
    all_to_all x1, waiting for transfers between devices, body(): recv = lax.all_to_all(placed, 'chip', 0, 0).reshape(chips * slots, 128)  12.3 us
    all_to_all x1, starting transfers between devices, body(): recv = lax.all_to_all(placed, 'chip', 0, 0).reshape(chips * slots, 128)  11 us
    all_to_all x1, waiting for transfers between devices, body(): got = lax.all_to_all(parts, 'chip', 0, 0)  10.8 us
    all_to_all x1, waiting for transfers between devices, body(): full = lax.all_to_all(out, 'chip', 0, 0)  10.7 us
    all_gather x1, blocking collectives, body(): lax.all_gather(recv[:, dates:dates + shard].T, 'rhs', axis=0, tiled=True)  9.72 us
    all_gather x1, blocking collectives, body(): pair = lax.all_gather(payload, 'core', axis=0, tiled=False)  8.45 us
    all_gather x1, blocking collectives, body(): both = lax.all_gather(update, 'core', axis=0, tiled=True)  7.62 us
    all_gather x1, blocking collectives, body(): full = lax.all_gather(full, 'core', axis=0, tiled=True)  5.16 us
  transfers between devices with their start and end apart: 3, of which 3 were waited for; matrix products, arithmetic and copies ran while one was open for 3% of the time, Pallas kernels for 0%

profile of v1, /device:TPU:1, one launch (start us, length us, event | category | flops | bytes accessed | tf_op | source)
XLA Modules:
  0.0 99.8 jit_solution(17323923745384394983)
XLA Ops:
  0.6 0.0 copy-start
  0.7 0.9 select_reduce_fusion
  1.6 0.2 convert_reduce_fusion
  1.8 1.7 %concatenate.3 = f32[120,256]{1,0:T(8,128)S(1)} concatenate(f32[80,256]{1,0:T(8,128)} %param.10, f32[32,256]{1,0:T(8,128)} %param.9, f32[1,256]{1,0:T(1,128)S(1)} %get-tuple-element.3, f32[1,256]{1,0:T(1,128)S(1)} %get-tuple-element.2, f32[6,256]{1,0:T(8,128)S(1)} %broadcast_in_dim.32), dimensions={0} | concatenate | bytes 245760 | tf_op jit(solution)/shard_map/concatenate | solution.py:39
  3.5 8.4 %all-gather = f32[240,256]{1,0:T(8,128)S(1)} all-gather(f32[120,256]{1,0:T(8,128)S(1)} %concatenate.3), channel_id=2, replica_groups=mesh['chip'=64,'core'=2,'rhs'=4] {'core'}, dimensions={0}, use_global_device_ids=true | all-gather | bytes 368640 | tf_op jit(solution)/shard_map/all_gather | solution.py:40
  12.0 0.6 convolution_bitcast_fusion
  12.6 0.0 copy-start.4
  12.6 0.0 copy-start.5
  12.6 0.0 copy-start.1
  12.7 0.0 copy-start.3
  12.7 0.7 pad_bitcast_fusion
  13.4 11.0 %all-to-all-start = ((f32[64,8,128]{2,1,0:T(8,128)}), f32[64,8,128]{2,1,0:T(8,128)S(1)}, u32[]{:S(2)}, u32[]{:S(2)}) async-start(f32[64,8,128]{2,1,0:T(8,128)} %pad_bitcast_fusion), calls=%async_computation | async-start | bytes 524288 | tf_op jit(solution)/shard_map/all_to_all | solution.py:46
  24.4 0.0 copy-done.4
  24.4 0.0 copy-done.5
  24.4 0.2 select_reduce_fusion.1
  24.6 0.1 dynamic_slice.10
  24.7 0.1 compare_convert_fusion.1
  24.7 0.0 copy-done.1
  24.7 0.0 copy-done.3
  24.7 0.4 fusion.21
  25.1 12.3 %all-to-all-done = f32[64,8,128]{2,1,0:T(8,128)S(1)} async-done(((f32[64,8,128]{2,1,0:T(8,128)}), f32[64,8,128]{2,1,0:T(8,128)S(1)}, u32[]{:S(2)}, u32[]{:S(2)}) %all-to-all-start) | async-done | bytes 262176 | tf_op jit(solution)/shard_map/all_to_all | solution.py:46
  37.4 0.1 slice.19
  37.6 0.2 slice_reduce_fusion
  37.8 0.1 copy.46
  37.9 9.7 %all_gather.17 = f32[128,512]{1,0:T(8,128)S(1)} all-gather(f32[32,512]{1,0:T(8,128)S(1)} %bitcast.54), channel_id=1, replica_groups=mesh['chip'=64,'core'=2,'rhs'=4] {'rhs'}, dimensions={0}, use_global_device_ids=true | all-gather | bytes 327680 | tf_op jit(solution)/shard_map/all_gather | solution.py:47
  47.7 0.1 copy.37
  47.8 0.1 compare_convert_fusion
  47.9 0.7 fusion.1
  48.5 0.6 fusion.22
  49.2 7.6 %all_gather.18 = f32[8,80,128]{2,1,0:T(8,128)S(1)} all-gather(f32[4,80,128]{2,1,0:T(8,128)S(1)} %fusion.22), channel_id=1, replica_groups=mesh['chip'=64,'core'=2,'rhs'=4] {'core'}, dimensions={0}, use_global_device_ids=true | all-gather | bytes 491520 | tf_op jit(solution)/shard_map/all_gather | solution.py:57
  56.8 0.1 multiply_reduce_fusion.1
  56.9 0.1 copy.39
  57.0 0.8 all_to_all.20
  57.8 4.6 %all-to-all-start.1 = ((f32[64,1,640]{2,1,0:T(1,128)}), f32[64,1,640]{2,1,0:T(1,128)S(1)}, u32[]{:S(2)}, u32[]{:S(2)}) async-start(f32[64,1,640]{2,1,0:T(1,128)} %all_to_all.20), calls=%async_computation.1 | async-start | bytes 327680 | tf_op jit(solution)/shard_map/all_to_all | solution.py:71
  62.5 0.1 fusion.13
  62.5 0.0 copy-done
  62.5 1.0 %fusion.23 = f32[8,128,128]{2,1,0:T(8,128)S(1)} fusion(f32[8,128,128]{2,1,0:T(8,128)S(1)} %copy-done), kind=kOutput, calls=%fused_computation.60 | convolution fusion | flops 201326592 | bytes 1048576 | tf_op jit(solution)/shard_map/pdc,pde->pce/dot_general | solution.py:76
  63.6 10.8 %all-to-all-done.1 = f32[64,1,640]{2,1,0:T(1,128)S(1)} async-done(((f32[64,1,640]{2,1,0:T(1,128)}), f32[64,1,640]{2,1,0:T(1,128)S(1)}, u32[]{:S(2)}, u32[]{:S(2)}) %all-to-all-start.1) | async-done | bytes 163872 | tf_op jit(solution)/shard_map/all_to_all | solution.py:71
  74.4 0.1 reduce_sum.64
  74.5 0.7 dynamic-slice_subtract_fusion
  75.2 0.2 convolution_bitcast_fusion.1
  75.4 0.8 broadcast_in_dim.36
  76.2 4.7 %all-to-all-start.2 = ((f32[64,1,640]{2,1,0:T(1,128)}), f32[64,1,640]{2,1,0:T(1,128)S(1)}, u32[]{:S(2)}, u32[]{:S(2)}) async-start(f32[64,1,640]{2,1,0:T(1,128)} %broadcast_in_dim.36), calls=%async_computation.2 | async-start | bytes 327680 | tf_op jit(solution)/shard_map/all_to_all | solution.py:83
  80.8 0.6 fusion.19
  81.5 0.4 fusion.20
  81.8 10.7 %all-to-all-done.2 = f32[64,1,640]{2,1,0:T(1,128)S(1)} async-done(((f32[64,1,640]{2,1,0:T(1,128)}), f32[64,1,640]{2,1,0:T(1,128)S(1)}, u32[]{:S(2)}, u32[]{:S(2)}) %all-to-all-start.2) | async-done | bytes 163872 | tf_op jit(solution)/shard_map/all_to_all | solution.py:83
  92.6 5.2 %all-gather.1 = f32[128,1,640]{2,1,0:T(1,128)S(1)} all-gather(f32[64,1,640]{2,1,0:T(1,128)S(1)} %all-to-all-done.2), channel_id=3, replica_groups=mesh['chip'=64,'core'=2,'rhs'=4] {'core'}, dimensions={0}, use_global_device_ids=true | all-gather | bytes 491520 | tf_op jit(solution)/shard_map/all_gather | solution.py:84
  97.7 0.8 reduce.2
  98.5 0.1 reshape.333
  98.5 0.1 copy.42
  98.6 0.0 copy-start.2
  98.6 0.2 multiply_reduce_fusion
  98.8 1.0 %convolution_subtract_fusion = f32[4,80,128]{2,1,0:T(8,128)} fusion(f32[4,80,128]{2,1,0:T(8,128)S(1)} %fusion.20, f32[4,80,128]{2,1,0:T(8,128)S(1)} %multiply_reduce_fusion, f32[4,128,128]{2,1,0:T(8,128)S(1)} %fusion.21), kind=kOutput, calls=%fused_computation.3 | convolution fusion | flops 62955520 | bytes 753664 | tf_op jit(solution)/shard_map/ltc,lcd->ltd/dot_general | solution.py:91
  99.8 0.0 copy-done.2
  (11 shorter events, 0.1 us)
Async XLA Ops:
  0.6 61.9 %copy-start = (f32[8,128,128]{2,1,0:T(8,128)S(1)}, f32[8,128,128]{2,1,0:T(8,128)}, u32[]{:S(2)}) copy-start(f32[8,128,128]{2,1,0:T(8,128)} %param.16) | copy-start | bytes 1572868
  12.6 11.8 %copy-start.4 = (s32[512]{0:T(512)S(1)}, s32[512]{0:T(512)}, u32[]{:S(2)}) copy-start(s32[512]{0:T(512)} %param.12) | copy-start | bytes 6148
  12.6 11.8 %copy-start.5 = (s32[512]{0:T(512)S(1)}, s32[512]{0:T(512)}, u32[]{:S(2)}) copy-start(s32[512]{0:T(512)} %param.13) | copy-start | bytes 6148
  12.6 12.1 %copy-start.1 = (f32[4,128,128]{2,1,0:T(8,128)S(1)}, f32[4,128,128]{2,1,0:T(8,128)}, u32[]{:S(2)}) copy-start(f32[4,128,128]{2,1,0:T(8,128)} %param.14) | copy-start | bytes 786436
  12.7 12.1 %copy-start.3 = (f32[4,128,128]{2,1,0:T(8,128)S(1)}, f32[4,128,128]{2,1,0:T(8,128)}, u32[]{:S(2)}) copy-start(f32[4,128,128]{2,1,0:T(8,128)} %param.15) | copy-start | bytes 786436
  13.4 24.1 %all-to-all-start = ((f32[64,8,128]{2,1,0:T(8,128)}), f32[64,8,128]{2,1,0:T(8,128)S(1)}, u32[]{:S(2)}, u32[]{:S(2)}) async-start(f32[64,8,128]{2,1,0:T(8,128)} %pad_bitcast_fusion), calls=%async_computation | async-start | bytes 524288 | tf_op jit(solution)/shard_map/all_to_all | solution.py:46
  57.8 16.5 %all-to-all-start.1 = ((f32[64,1,640]{2,1,0:T(1,128)}), f32[64,1,640]{2,1,0:T(1,128)S(1)}, u32[]{:S(2)}, u32[]{:S(2)}) async-start(f32[64,1,640]{2,1,0:T(1,128)} %all_to_all.20), calls=%async_computation.1 | async-start | bytes 327680 | tf_op jit(solution)/shard_map/all_to_all | solution.py:71
  76.2 16.4 %all-to-all-start.2 = ((f32[64,1,640]{2,1,0:T(1,128)}), f32[64,1,640]{2,1,0:T(1,128)S(1)}, u32[]{:S(2)}, u32[]{:S(2)}) async-start(f32[64,1,640]{2,1,0:T(1,128)} %broadcast_in_dim.36), calls=%async_computation.2 | async-start | bytes 327680 | tf_op jit(solution)/shard_map/all_to_all | solution.py:83
  98.6 1.2 %copy-start.2 = (f32[8,5,16,128]{3,2,1,0:T(8,128)}, f32[8,5,16,128]{3,2,1,0:T(8,128)S(1)}, u32[]{:S(2)}) copy-start(f32[8,5,16,128]{3,2,1,0:T(8,128)S(1)} %copy.42) | copy-start | bytes 983044

commit v2 on v1

v2 whole, which is shorter than its diff:
```python
import jax
import jax.numpy as jnp
from jax import lax
from jax.experimental import pallas as pl
from jax.experimental.pallas import tpu as pltpu
from jax.sharding import Mesh, PartitionSpec as P

HI = lax.Precision.HIGHEST
CAP = 4
LANES = 128
NT = (((1,), (1,)), ((), ()))
NN = (((1,), (0,)), ((), ()))


def split3(x):
    hi = x.astype(jnp.bfloat16)
    rest = x - hi.astype(jnp.float32)
    mid = rest.astype(jnp.bfloat16)
    low = (rest - mid.astype(jnp.float32)).astype(jnp.bfloat16)
    return hi, mid, low


def pack_kernel(core_ref, map_ref, target_ref, data_ref, coef_ref, out_ref, feat_ref, *, local):
    cores, rows = target_ref.shape
    total = map_ref.shape[1]
    dates = data_ref.shape[1]
    shard = coef_ref.shape[1]
    slots = cores * CAP
    n_slots = out_ref.shape[0]
    owners = total // local
    f32, bf16, i32 = jnp.float32, jnp.bfloat16, jnp.int32
    own = core_ref[0]
    where_to = map_ref[...]
    owner_of = where_to // local
    table = jnp.concatenate(
        [owner_of, where_to % local] + [jnp.zeros((1, total), i32)] * 6, axis=0
    ).astype(f32).astype(bf16)
    ids = lax.broadcasted_iota(i32, (total, rows), 0)
    owner_ids = lax.broadcasted_iota(i32, (owners, rows), 0)
    before = (
        lax.broadcasted_iota(i32, (rows, rows), 0) < lax.broadcasted_iota(i32, (rows, rows), 1)
    ).astype(f32).astype(bf16)
    feat_ref[...] = jnp.zeros(feat_ref.shape, f32)
    codes = []
    for s in range(cores):
        hit = (ids == target_ref[s : s + 1, :]).astype(f32).astype(bf16)
        found = lax.dot_general(table, hit, NN, preferred_element_type=f32)
        owner = found[0:1, :].astype(i32)
        same = (owner_ids == owner).astype(f32)
        count = lax.dot_general(same.astype(bf16), before, NN, preferred_element_type=f32)
        rank = jnp.sum(same * count, axis=0, keepdims=True).astype(i32)
        slot = (owner // cores) * slots + s * CAP + rank
        codes.append(jnp.where(owner % cores == own, slot, -1))
        cols = slice(s * rows, (s + 1) * rows)
        feat_ref[0:dates, cols] = data_ref[s]
        feat_ref[dates : dates + shard, cols] = coef_ref[s]
        feat_ref[dates + shard : dates + shard + 1, cols] = found[1:2, :] + 1.0
    code = jnp.concatenate(codes, axis=1)
    put = (lax.broadcasted_iota(i32, (n_slots, cores * rows), 0) == code).astype(f32).astype(bf16)
    acc = None
    for part in split3(feat_ref[...]):
        term = lax.dot_general(put, part, NT, preferred_element_type=f32)
        acc = term if acc is None else acc + term
    out_ref[...] = acc


def turn_kernel(recv_ref, turned_ref, share_ref, *, dates):
    turned = recv_ref[...].T
    turned_ref[...] = turned
    shard = share_ref.shape[1]
    for i in range(share_ref.shape[0]):
        share_ref[i] = turned[dates : dates + shard, :]


def forward_kernel(turned_ref, coef_ref, comb_ref, rhs_ref, update_ref, *, shard):
    local, dates, _ = rhs_ref.shape
    data = turned_ref[0:dates, :]
    mark = turned_ref[dates + shard : dates + shard + 1, :]
    coef = coef_ref[...]
    for k in range(local):
        picked = jnp.where(mark == float(k + 1), data, 0.0)
        rhs = lax.dot_general(picked, coef, NT, precision=HI, preferred_element_type=jnp.float32)
        rhs_ref[k] = rhs
        update_ref[k] = lax.dot_general(
            rhs, comb_ref[k], NT, precision=HI, preferred_element_type=jnp.float32
        )


def middle_kernel(got_ref, rhs_ref, gram_ref, out_ref):
    pieces, width = rhs_ref.shape
    chips = got_ref.shape[0] // pieces
    sums = [
        jnp.sum(got_ref[pl.ds(k, chips, stride=pieces), :], axis=0, keepdims=True)
        for k in range(pieces)
    ]
    left = rhs_ref[...] - jnp.concatenate(sums, axis=0)
    left = jnp.concatenate([left, jnp.zeros((8 - pieces % 8, width), jnp.float32)], axis=0)
    sol = lax.dot_general(
        left, gram_ref[...], NN, precision=HI, preferred_element_type=jnp.float32
    )
    for k in range(pieces):
        out_ref[pl.ds(k, chips, stride=pieces), :] = jnp.broadcast_to(
            sol[k : k + 1, :], (chips, width)
        )


def last_kernel(parent_ref, top_ref, base_ref, comb_ref, out_ref):
    for k in range(out_ref.shape[0]):
        lifted = lax.dot_general(
            top_ref[parent_ref[k]],
            comb_ref[k],
            NN,
            precision=HI,
            preferred_element_type=jnp.float32,
        )
        out_ref[k] = base_ref[k] - lifted


VM = pl.BlockSpec(memory_space=pltpu.VMEM)
SM = pl.BlockSpec(memory_space=pltpu.SMEM)


def arr(*shape):
    return pltpu.VMEM(shape, jnp.float32)


def vmem(*arrays):
    return [pltpu.with_memory_space_constraint(a, pltpu.VMEM) for a in arrays]


def body(
    obs_coef, obs_data, obs_target, leaf_map, leaf_parent, leaf_inv, leaf_off, top_inv, top_rhs
):
    chips = lax.axis_size("chip")
    cores = lax.axis_size("core")
    planes = lax.axis_size("rhs")
    q = lax.axis_index("chip")
    c = lax.axis_index("core")
    local = leaf_inv.shape[0]
    width = leaf_inv.shape[1]
    tops = top_inv.shape[0]
    dates = obs_data.shape[0]
    shard = obs_coef.shape[0]
    total = leaf_map.shape[0]
    slots = cores * CAP
    n_slots = chips * slots
    half = tops // cores
    pieces = half * dates // chips
    span = dates // pieces

    pair_target = lax.all_gather(obs_target, "core", axis=0)
    pair_data = lax.all_gather(obs_data, "core", axis=0)
    pair_coef = lax.all_gather(obs_coef, "core", axis=0)
    rows = cores * obs_target.shape[0]
    placed = pl.pallas_call(
        lambda *refs: pack_kernel(*refs, local=local),
        out_shape=arr(n_slots, LANES),
        in_specs=[SM, VM, VM, VM, VM],
        out_specs=VM,
        scratch_shapes=[pltpu.VMEM((LANES, rows), jnp.float32)],
        name="pack",
    )(c.reshape(1), *vmem(leaf_map.reshape(1, total), pair_target, pair_data, pair_coef))
    recv = lax.all_to_all(placed.reshape(chips, slots, LANES), "chip", 0, 0)
    turned, share = pl.pallas_call(
        lambda *refs: turn_kernel(*refs, dates=dates),
        out_shape=(arr(LANES, n_slots), arr(planes, shard, n_slots)),
        in_specs=[VM],
        out_specs=(VM, VM),
        name="turn",
    )(*vmem(recv.reshape(n_slots, LANES)))
    coef = lax.all_to_all(share, "rhs", 0, 0).reshape(planes * shard, n_slots)
    comb = jnp.einsum("lcd,lde->lce", leaf_off, leaf_inv, precision=HI)
    rhs, update = pl.pallas_call(
        lambda *refs: forward_kernel(*refs, shard=shard),
        out_shape=(arr(local, dates, width), arr(local, dates, width)),
        in_specs=[VM, VM, VM],
        out_specs=(VM, VM),
        name="forward",
    )(*vmem(turned, coef, comb))
    both = lax.all_gather(update, "core", axis=0, tiled=True)

    first = q * cores * local
    places = first + jnp.arange(cores * local, dtype=jnp.int32)
    held = leaf_map[None, :] == places[:, None]
    parent = jnp.sum(jnp.where(held, leaf_parent[None, :], 0), axis=1)
    mine = c * half + jnp.arange(half, dtype=jnp.int32)
    to_top = (parent[None, :] == mine[:, None]).astype(jnp.float32)
    contrib = jnp.sum(to_top[:, :, None, None] * both[None], axis=1)
    parts = contrib.reshape(chips, 1, pieces * width)
    got = lax.all_to_all(parts, "chip", 0, 0)

    p = c * half + q // span
    own_inv = lax.dynamic_index_in_dim(top_inv, p, 0, keepdims=False)
    gram = lax.dot_general(own_inv, own_inv, (((0,), (0,)), ((), ())), precision=HI)
    own_rhs = lax.dynamic_slice(top_rhs, (p, (q % span) * pieces, 0), (1, pieces, width))
    out = pl.pallas_call(
        middle_kernel,
        out_shape=arr(chips * pieces, width),
        in_specs=[VM, VM, VM],
        out_specs=VM,
        name="middle",
    )(*vmem(got.reshape(chips * pieces, width), own_rhs.reshape(pieces, width), gram))
    full = lax.all_to_all(out.reshape(chips, 1, pieces * width), "chip", 0, 0)
    full = lax.all_gather(full.reshape(half, dates, width), "core", axis=0, tiled=True)

    solved = jnp.einsum("ltc,ldc->ltd", rhs, leaf_inv, precision=HI)
    base = jnp.einsum("ltc,lcd->ltd", solved, leaf_inv, precision=HI)
    leaf_solution = pl.pallas_call(
        last_kernel,
        out_shape=jax.ShapeDtypeStruct((local, dates, width), jnp.float32),
        in_specs=[SM, VM, VM, VM],
        out_specs=VM,
        name="last",
    )(lax.dynamic_slice_in_dim(parent, c * local, local, 0), *vmem(full, base, comb))
    return (leaf_solution, full)


def solution(mesh):
    devices = mesh.devices
    split = Mesh(devices.reshape(devices.shape[0] // 2, 2, -1), ("chip", "core", "rhs"))
    leaf = ("chip", "core")
    return jax.shard_map(
        body,
        mesh=split,
        in_specs=(
            P("rhs", leaf),
            P("rhs", leaf),
            P(leaf),
            P(),
            P(),
            P(leaf, None, None),
            P(leaf, None, None),
            P(),
            P(None, "rhs", None),
        ),
        out_specs=(P(leaf, "rhs", None), P(None, "rhs", None)),
        check_vma=False,
    )
```

time: 100 us -> 102 us (1.020)
  Pallas kernels: 0 us -> 8.03 us
  blocking collectives: 30.9 us -> 24 us
  waiting for transfers between devices: 33.8 us -> 38.9 us
  starting transfers between devices: 20.2 us -> 24.3 us
  matrix products: 5.52 us -> 1.67 us
  other arithmetic: 3.51 us -> 1.08 us
  local copies, waits for them, and re-layouts: 4.93 us -> 2.73 us
    pallas_call x0 -> x5, Pallas kernels: none -> 8.03 us  [the longest x1 2.87 us: body(): pl.pallas_call(lambda *refs: forward_kernel(*refs, shard=shard), out_shap...]
    all_to_all x2 -> x3, waiting for transfers between devices: 23 us -> 28.6 us  [the longest x1 12.4 us: body(): recv = lax.all_to_all(placed.reshape(chips, slots, LANES), 'chip', 0, 0)]
    all_gather x3 -> x4, blocking collectives: 23.3 us -> 18.1 us  [the longest x1 8.65 us: body(): pair_target = lax.all_gather(obs_target, 'core', axis=0)]
    all_to_all x2 -> x3, starting transfers between devices: 15.6 us -> 19.7 us  [the longest x1 11 us: body(): recv = lax.all_to_all(placed.reshape(chips, slots, LANES), 'chip', 0, 0)]
    dot_general x6 -> x1, matrix products: 4.14 us -> 0.28 us  [body(): lax.dot_general(own_inv, own_inv, (((0,), (0,)), ((), ())), precision=HI)]
    all_gather x1, blocking collectives: 7.62 us -> 5.9 us  [body(): both = lax.all_gather(update, 'core', axis=0, tiled=True)]
    concatenate x1 -> x0, local copies, waits for them, and re-layouts: 1.68 us -> none  [body(): payload = jnp.concatenate([obs_data, obs_coef, meta, pad], axis=0)]
    reduce_sum x4 -> x0, other arithmetic: 1.4 us -> none  [the longest x1 0.95 us: body(): jnp.sum(jnp.where(obs_target[:, None] == ids[None, :], leaf_map[None, :],...]
  transfers between devices with their start and end apart: 3 -> 4, of which waited for: 3 -> 4; matrix products, arithmetic and copies ran while one was open for 3% -> 3% of each run, Pallas kernels for 0% -> 0%
where the time goes in v2:
time: 102 us; the launch traced here: 101 us
  waiting for transfers between devices  38.9 us (38%)
  starting transfers between devices  24.3 us (24%)
  blocking collectives  24 us (24%)
  Pallas kernels  8.03 us (8%)
  local copies, waits for them, and re-layouts  2.73 us (3%)
  matrix products  1.67 us (2%)
  other arithmetic  1.08 us (1%)
    all_to_all x1, waiting for transfers between devices, body(): recv = lax.all_to_all(placed.reshape(chips, slots, LANES), 'chip', 0, 0)  12.4 us
    all_to_all x1, starting transfers between devices, body(): recv = lax.all_to_all(placed.reshape(chips, slots, LANES), 'chip', 0, 0)  11 us
    all_to_all x1, waiting for transfers between devices, body(): full = lax.all_to_all(out.reshape(chips, 1, pieces * width), 'chip', 0, 0)  10.7 us
    all_to_all x1, waiting for transfers between devices, body(): got = lax.all_to_all(parts, 'chip', 0, 0)  10.3 us
    all_gather x1, blocking collectives, body(): pair_target = lax.all_gather(obs_target, 'core', axis=0)  8.65 us
    all_gather x1, blocking collectives, body(): both = lax.all_gather(update, 'core', axis=0, tiled=True)  5.9 us
    all_to_all x1, waiting for transfers between devices, body(): coef = lax.all_to_all(share, 'rhs', 0, 0).reshape(planes * shard, n_slots)  5.46 us
    all_gather x1, blocking collectives, body(): lax.all_gather(full.reshape(half, dates, width), 'core', axis=0, tiled=True)  5.16 us
  transfers between devices with their start and end apart: 4, of which 4 were waited for; matrix products, arithmetic and copies ran while one was open for 3% of the time, Pallas kernels for 0%

profile of v2, /device:TPU:1, one launch (start us, length us, event | category | flops | bytes accessed | tf_op | source)
XLA Modules:
  0.0 101.5 jit_solution(3853793643074933167)
XLA Ops:
  0.6 0.0 copy-start
  0.7 8.6 %all-gather.3 = s32[2,1,256]{2,1,0:T(1,128)S(1)} all-gather(s32[1,1,256]{2,1,0:T(1,128)} %bitcast.34), channel_id=2, replica_groups=mesh['chip'=64,'core'=2,'rhs'=4] {'core'}, dimensions={0}, use_global_device_ids=true | all-gather | bytes 3072 | tf_op jit(solution)/shard_map/all_gather | solution.py:151
  9.3 0.0 copy-start.2
  9.3 2.3 %all-gather.1 = f32[160,256]{1,0:T(8,128)S(1)} all-gather(f32[80,256]{1,0:T(8,128)} %param.10), channel_id=3, replica_groups=mesh['chip'=64,'core'=2,'rhs'=4] {'core'}, dimensions={0}, use_global_device_ids=true | all-gather | bytes 245760 | tf_op jit(solution)/shard_map/all_gather | solution.py:152
  11.6 2.1 %all-gather.2 = f32[64,256]{1,0:T(8,128)S(1)} all-gather(f32[32,256]{1,0:T(8,128)} %param.9), channel_id=4, replica_groups=mesh['chip'=64,'core'=2,'rhs'=4] {'core'}, dimensions={0}, use_global_device_ids=true | all-gather | bytes 98304 | tf_op jit(solution)/shard_map/all_gather | solution.py:153
  13.6 0.0 copy-start.4
  13.6 0.0 copy-start.1
  13.6 0.7 copy-done.1
  14.3 0.0 copy-start.3
  14.3 1.8 %pack.1 = f32[512,128]{1,0:T(8,128)} custom-call(s32[1]{0:T(128)} %bitcast.refs_0_, s32[1,512]{1,0:T(1,128)S(1)} %bitcast.31, s32[2,256]{1,0:T(2,128)S(1)} %bitcast.32, f32[2,80,256]{2,1,0:T(8,128)S(1)} %bitcast.29, f32[2,32,256]{2,1,0:T(8,128)S(1)} %bitcast.30), custom_call_target="tpu_custom_call" | custom-call | tf_op jit(solution)/shard_map/pack/pallas_call | solution.py:155
  16.1 11.0 %all-to-all-start = ((f32[64,8,128]{2,1,0:T(8,128)}), f32[64,8,128]{2,1,0:T(8,128)S(1)}, u32[]{:S(2)}, u32[]{:S(2)}) async-start(f32[64,8,128]{2,1,0:T(8,128)} %bitcast.5), calls=%async_computation | async-start | bytes 524288 | tf_op jit(solution)/shard_map/all_to_all | solution.py:163
  27.1 0.0 copy-done.4
  27.1 0.2 select_reduce_fusion
  27.3 0.0 copy-done.2
  27.3 0.0 copy-done.3
  27.3 0.4 fusion.4.refs_2_.comb_ref
  27.7 12.4 %all-to-all-done = f32[64,8,128]{2,1,0:T(8,128)S(1)} async-done(((f32[64,8,128]{2,1,0:T(8,128)}), f32[64,8,128]{2,1,0:T(8,128)S(1)}, u32[]{:S(2)}, u32[]{:S(2)}) %all-to-all-start) | async-done | bytes 262176 | tf_op jit(solution)/shard_map/all_to_all | solution.py:163
  40.2 0.8 turn.1
  41.0 4.0 %all-to-all-start.1 = ((f32[4,32,512]{2,1,0:T(8,128)}), f32[4,32,512]{2,1,0:T(8,128)S(1)}, u32[]{:S(2)}, u32[]{:S(2)}) async-start(f32[4,32,512]{2,1,0:T(8,128)} %get-tuple-element.7), calls=%async_computation.1 | async-start | bytes 524288 | tf_op jit(solution)/shard_map/all_to_all | solution.py:171
  45.0 0.1 compare_convert_fusion
  45.1 5.5 %all-to-all-done.1 = f32[4,32,512]{2,1,0:T(8,128)S(1)} async-done(((f32[4,32,512]{2,1,0:T(8,128)}), f32[4,32,512]{2,1,0:T(8,128)S(1)}, u32[]{:S(2)}, u32[]{:S(2)}) %all-to-all-start.1) | async-done | bytes 262176 | tf_op jit(solution)/shard_map/all_to_all | solution.py:171
  50.6 2.9 %forward.1 = (f32[4,80,128]{2,1,0:T(8,128)S(1)}, f32[4,80,128]{2,1,0:T(8,128)S(1)}) custom-call(f32[128,512]{1,0:T(8,128)S(1)} %get-tuple-element.6.refs_0_, f32[128,512]{1,0:T(8,128)S(1)} %bitcast.26, f32[4,128,128]{2,1,0:T(8,128)S(1)} %fusion.4.refs_2_.comb_ref), custom_call_target="tpu_custom_call" | custom-call | tf_op jit(solution)/shard_map/forward/pallas_call | solution.py:173
  53.4 5.9 %all_gather.30 = f32[8,80,128]{2,1,0:T(8,128)S(1)} all-gather(f32[4,80,128]{2,1,0:T(8,128)S(1)} %get-tuple-element.8), channel_id=1, replica_groups=mesh['chip'=64,'core'=2,'rhs'=4] {'core'}, dimensions={0}, use_global_device_ids=true | all-gather | bytes 491520 | tf_op jit(solution)/shard_map/all_gather | solution.py:180
  59.3 0.8 multiply_reduce_fusion
  60.1 4.6 %all-to-all-start.2 = ((f32[64,1,640]{2,1,0:T(1,128)}), f32[64,1,640]{2,1,0:T(1,128)S(1)}, u32[]{:S(2)}, u32[]{:S(2)}) async-start(f32[64,1,640]{2,1,0:T(1,128)} %bitcast.8), calls=%async_computation.2 | async-start | bytes 327680 | tf_op jit(solution)/shard_map/all_to_all | solution.py:190
  64.8 0.6 dynamic_slice.10.parent_ref
  65.4 0.7 dynamic-slice_bitcast_fusion.rhs_ref
  66.1 0.0 copy-done
  66.1 0.3 fusion.gram_ref
  66.4 10.3 %all-to-all-done.2 = f32[64,1,640]{2,1,0:T(1,128)S(1)} async-done(((f32[64,1,640]{2,1,0:T(1,128)}), f32[64,1,640]{2,1,0:T(1,128)S(1)}, u32[]{:S(2)}, u32[]{:S(2)}) %all-to-all-start.2) | async-done | bytes 163872 | tf_op jit(solution)/shard_map/all_to_all | solution.py:190
  76.7 0.9 middle.1
  77.5 4.7 %all-to-all-start.3 = ((f32[64,1,640]{2,1,0:T(1,128)}), f32[64,1,640]{2,1,0:T(1,128)S(1)}, u32[]{:S(2)}, u32[]{:S(2)}) async-start(f32[64,1,640]{2,1,0:T(1,128)} %bitcast.12), calls=%async_computation.3 | async-start | bytes 327680 | tf_op jit(solution)/shard_map/all_to_all | solution.py:203
  82.2 0.6 fusion.5
  82.8 0.4 fusion.6.base_ref
  83.2 10.7 %all-to-all-done.3 = f32[64,1,640]{2,1,0:T(1,128)S(1)} async-done(((f32[64,1,640]{2,1,0:T(1,128)}), f32[64,1,640]{2,1,0:T(1,128)S(1)}, u32[]{:S(2)}, u32[]{:S(2)}) %all-to-all-start.3) | async-done | bytes 163872 | tf_op jit(solution)/shard_map/all_to_all | solution.py:203
  93.9 5.2 %all_gather.31.top_ref = f32[8,80,128]{2,1,0:T(8,128)S(1)} all-gather(f32[4,80,128]{2,1,0:T(8,128)S(1)} %bitcast.33), channel_id=1, replica_groups=mesh['chip'=64,'core'=2,'rhs'=4] {'core'}, dimensions={0}, use_global_device_ids=true | all-gather | bytes 491520 | tf_op jit(solution)/shard_map/all_gather | solution.py:204
  99.1 1.7 %last.1 = f32[4,80,128]{2,1,0:T(8,128)} custom-call(s32[4]{0:T(128)} %dynamic_slice.10.parent_ref, f32[8,80,128]{2,1,0:T(8,128)S(1)} %all_gather.31.top_ref, f32[4,80,128]{2,1,0:T(8,128)S(1)} %fusion.6.base_ref, f32[4,128,128]{2,1,0:T(8,128)S(1)} %fusion.4.refs_2_.comb_ref), custom_call_target="tpu_custom_call" | custom-call | tf_op jit(solution)/shard_map/last/pallas_call | solution.py:208
  100.7 0.7 copy.18
  (3 shorter events, 0.0 us)
Async XLA Ops:
  0.6 65.5 %copy-start = (f32[8,128,128]{2,1,0:T(8,128)S(1)}, f32[8,128,128]{2,1,0:T(8,128)}, u32[]{:S(2)}) copy-start(f32[8,128,128]{2,1,0:T(8,128)} %param.16) | copy-start | bytes 1572868
  9.3 18.0 %copy-start.2 = (f32[4,128,128]{2,1,0:T(8,128)S(1)}, f32[4,128,128]{2,1,0:T(8,128)}, u32[]{:S(2)}) copy-start(f32[4,128,128]{2,1,0:T(8,128)} %param.14) | copy-start | bytes 786436
  13.6 13.5 %copy-start.4 = (s32[512]{0:T(512)S(1)}, s32[512]{0:T(512)}, u32[]{:S(2)}) copy-start(s32[512]{0:T(512)} %param.13) | copy-start | bytes 6148
  13.6 0.7 copy-start.1
  14.3 13.0 %copy-start.3 = (f32[4,128,128]{2,1,0:T(8,128)S(1)}, f32[4,128,128]{2,1,0:T(8,128)}, u32[]{:S(2)}) copy-start(f32[4,128,128]{2,1,0:T(8,128)} %param.15) | copy-start | bytes 786436
  16.1 24.1 %all-to-all-start = ((f32[64,8,128]{2,1,0:T(8,128)}), f32[64,8,128]{2,1,0:T(8,128)S(1)}, u32[]{:S(2)}, u32[]{:S(2)}) async-start(f32[64,8,128]{2,1,0:T(8,128)} %bitcast.5), calls=%async_computation | async-start | bytes 524288 | tf_op jit(solution)/shard_map/all_to_all | solution.py:163
  41.0 9.6 %all-to-all-start.1 = ((f32[4,32,512]{2,1,0:T(8,128)}), f32[4,32,512]{2,1,0:T(8,128)S(1)}, u32[]{:S(2)}, u32[]{:S(2)}) async-start(f32[4,32,512]{2,1,0:T(8,128)} %get-tuple-element.7), calls=%async_computation.1 | async-start | bytes 524288 | tf_op jit(solution)/shard_map/all_to_all | solution.py:171
  60.1 16.5 %all-to-all-start.2 = ((f32[64,1,640]{2,1,0:T(1,128)}), f32[64,1,640]{2,1,0:T(1,128)S(1)}, u32[]{:S(2)}, u32[]{:S(2)}) async-start(f32[64,1,640]{2,1,0:T(1,128)} %bitcast.8), calls=%async_computation.2 | async-start | bytes 327680 | tf_op jit(solution)/shard_map/all_to_all | solution.py:190
  77.5 16.4 %all-to-all-start.3 = ((f32[64,1,640]{2,1,0:T(1,128)}), f32[64,1,640]{2,1,0:T(1,128)S(1)}, u32[]{:S(2)}, u32[]{:S(2)}) async-start(f32[64,1,640]{2,1,0:T(1,128)} %bitcast.12), calls=%async_computation.3 | async-start | bytes 327680 | tf_op jit(solution)/shard_map/all_to_all | solution.py:203

commit v3 on v2

v3 whole, which is shorter than its diff:
```python
import jax
import jax.numpy as jnp
from jax import lax
from jax.experimental import pallas as pl
from jax.experimental.pallas import tpu as pltpu
from jax.sharding import Mesh, PartitionSpec as P

HI = lax.Precision.HIGHEST
CAP = 4
LANES = 128
NT = (((1,), (1,)), ((), ()))
NN = (((1,), (0,)), ((), ()))
F32, BF16, I32 = jnp.float32, jnp.bfloat16, jnp.int32


def split2(x):
    high = x.astype(BF16)
    return high, (x - high.astype(F32)).astype(BF16)


def dot(a, b, dims):
    return lax.dot_general(a, b, dims, preferred_element_type=F32)


def join_kernel(
    map_hbm, target_hbm, data_hbm, coef_hbm, out_ref, map_ref, target_ref, sems, *, local, cores
):
    dates, rows = data_hbm.shape
    shard = coef_hbm.shape[0]
    total = map_hbm.shape[1]
    copies = [
        pltpu.make_async_copy(map_hbm, map_ref, sems.at[0]),
        pltpu.make_async_copy(target_hbm, target_ref, sems.at[1]),
        pltpu.make_async_copy(data_hbm, out_ref.at[pl.ds(0, dates)], sems.at[2]),
        pltpu.make_async_copy(coef_hbm, out_ref.at[pl.ds(dates, shard)], sems.at[3]),
    ]
    for copy in copies:
        copy.start()
    owners = total // local
    chips = owners // cores
    ids = lax.broadcasted_iota(I32, (total, rows), 0)
    owner_ids = lax.broadcasted_iota(I32, (owners, rows), 0)
    before = (
        lax.broadcasted_iota(I32, (rows, rows), 0) < lax.broadcasted_iota(I32, (rows, rows), 1)
    ).astype(F32).astype(BF16)
    copies[0].wait()
    copies[1].wait()
    where_to = map_ref[...]
    table = jnp.concatenate(
        [where_to // local, where_to % local] + [jnp.zeros((1, total), I32)] * 6, axis=0
    ).astype(F32).astype(BF16)
    hit = (ids == target_ref[...]).astype(F32).astype(BF16)
    found = dot(table, hit, NN)
    owner = found[0:1, :].astype(I32)
    same = (owner_ids == owner).astype(F32)
    rank = jnp.sum(same * dot(same.astype(BF16), before, NN), axis=0, keepdims=True)
    slot = (owner // cores) * (cores * CAP) + rank.astype(I32)
    code = (owner % cores) * (chips * cores * CAP) + slot + lax.axis_index("core") * CAP
    tail = out_ref.shape[0] - dates - shard
    out_ref[dates + shard :, :] = jnp.concatenate(
        [found[1:2, :] + 1.0, code.astype(F32), jnp.zeros((tail - 2, rows), F32)], axis=0
    )
    copies[2].wait()
    copies[3].wait()


def pack_kernel(pair_ref, out_ref, *, code_row):
    cores, height, rows = pair_ref.shape
    n_slots = out_ref.shape[0]
    code = jnp.concatenate([pair_ref[s, code_row : code_row + 1, :] for s in range(cores)], axis=1)
    code = code.astype(I32) - lax.axis_index("core") * n_slots
    put = (lax.broadcasted_iota(I32, (n_slots, cores * rows), 0) == code).astype(F32).astype(BF16)
    rest = jnp.zeros((LANES - height, cores * rows), F32)
    feat = jnp.concatenate([pair_ref[s] for s in range(cores)], axis=1)
    feat = jnp.concatenate([feat, rest], axis=0)
    both = dot(put, jnp.concatenate(split2(feat), axis=0), NT)
    out_ref[...] = both[:, :LANES] + both[:, LANES:]


def turn_kernel(recv_ref, turned_ref, share_ref, *, dates):
    turned = recv_ref[...].T
    turned_ref[...] = turned
    shard = share_ref.shape[1]
    for i in range(share_ref.shape[0]):
        share_ref[i] = turned[dates : dates + shard, :]


def forward_kernel(turned_ref, coef_ref, comb_ref, rhs_ref, update_ref, *, shard):
    local, dates, _ = rhs_ref.shape
    data = turned_ref[0:dates, :]
    mark = turned_ref[dates + shard : dates + shard + 1, :]
    coef_high, coef_low = split2(coef_ref[...])
    coef = jnp.concatenate([coef_high, coef_high, coef_low], axis=1)
    picked = jnp.concatenate(
        [jnp.where(mark == float(k + 1), data, 0.0) for k in range(local)], axis=0
    )
    high, low = split2(picked)
    rhs = dot(jnp.concatenate([high, low, high], axis=1), coef, NT)
    high, low = split2(rhs)
    rows = jnp.concatenate([high, low, high], axis=1)
    for k in range(local):
        part = slice(k * dates, (k + 1) * dates)
        rhs_ref[k] = rhs[part]
        update_ref[k] = dot(rows[part], comb_ref[k], NN)


def reduce_kernel(both_ref, parent_ref, out_ref):
    half, dates, width = out_ref.shape
    first = lax.axis_index("core") * half
    for p in range(half):
        acc = None
        for k in range(both_ref.shape[0]):
            term = jnp.where(parent_ref[k : k + 1, :] == first + p, both_ref[k], 0.0)
            acc = term if acc is None else acc + term
        out_ref[p] = acc


def middle_kernel(got_ref, rhs_ref, gram_ref, out_ref):
    pieces, width = rhs_ref.shape
    chips = got_ref.shape[0] // pieces
    sums = [
        jnp.sum(got_ref[pl.ds(k, chips, stride=pieces), :], axis=0, keepdims=True)
        for k in range(pieces)
    ]
    left = rhs_ref[...] - jnp.concatenate(sums, axis=0)
    left = jnp.concatenate([left, jnp.zeros((8 - pieces % 8, width), F32)], axis=0)
    high, low = split2(left)
    sol = dot(jnp.concatenate([high, low, high], axis=1), gram_ref[...], NN)
    for k in range(pieces):
        out_ref[pl.ds(k, chips, stride=pieces), :] = jnp.broadcast_to(
            sol[k : k + 1, :], (chips, width)
        )


def last_kernel(parent_ref, top_ref, base_ref, comb_ref, out_hbm, top_hbm, out_ref, sems):
    local = out_ref.shape[0]
    tops = top_ref.shape[0]
    copy_top = pltpu.make_async_copy(top_ref, top_hbm, sems.at[0])
    copy_top.start()
    copies = []
    for k in range(local):
        parent = parent_ref[k : k + 1, :]
        x = jnp.where(parent == 0, top_ref[0], 0.0)
        for p in range(1, tops):
            x = jnp.where(parent == p, top_ref[p], x)
        high, low = split2(x)
        lifted = dot(jnp.concatenate([high, low, high], axis=1), comb_ref[k], NN)
        out_ref[k] = base_ref[k] - lifted
        copies.append(pltpu.make_async_copy(out_ref.at[k], out_hbm.at[k], sems.at[1 + k]))
        copies[-1].start()
    copy_top.wait()
    for copy in copies:
        copy.wait()


VM = pl.BlockSpec(memory_space=pltpu.VMEM)
ANY = pl.BlockSpec(memory_space=pl.ANY)


def arr(*shape):
    return pltpu.VMEM(shape, F32)


def vmem(*arrays):
    return [pltpu.with_memory_space_constraint(a, pltpu.VMEM) for a in arrays]


def triple(m):
    high = lax.reduce_precision(m, 8, 7)
    low = (m - high).astype(BF16)
    high = high.astype(BF16)
    return jnp.concatenate([high, high, low], axis=-2)


def body(
    obs_coef, obs_data, obs_target, leaf_map, leaf_parent, leaf_inv, leaf_off, top_inv, top_rhs
):
    chips = lax.axis_size("chip")
    cores = lax.axis_size("core")
    planes = lax.axis_size("rhs")
    q = lax.axis_index("chip")
    c = lax.axis_index("core")
    local = leaf_inv.shape[0]
    width = leaf_inv.shape[1]
    tops = top_inv.shape[0]
    dates, rows = obs_data.shape
    shard = obs_coef.shape[0]
    total = leaf_map.shape[0]
    slots = cores * CAP
    n_slots = chips * slots
    half = tops // cores
    pieces = half * dates // chips
    span = dates // pieces
    height = dates + shard + 8

    payload = pl.pallas_call(
        lambda *refs: join_kernel(*refs, local=local, cores=cores),
        out_shape=arr(height, rows),
        in_specs=[ANY, ANY, ANY, ANY],
        out_specs=VM,
        scratch_shapes=[
            pltpu.VMEM((1, total), I32),
            pltpu.VMEM((1, rows), I32),
            pltpu.SemaphoreType.DMA((4,)),
        ],
        name="join",
    )(leaf_map.reshape(1, total), obs_target.reshape(1, rows), obs_data, obs_coef)
    pair = lax.all_gather(payload, "core", axis=0)
    placed = pl.pallas_call(
        lambda *refs: pack_kernel(*refs, code_row=dates + shard + 1),
        out_shape=arr(n_slots, LANES),
        in_specs=[VM],
        out_specs=VM,
        name="pack",
    )(*vmem(pair))
    recv = lax.all_to_all(placed.reshape(chips, slots, LANES), "chip", 0, 0)
    turned, share = pl.pallas_call(
        lambda *refs: turn_kernel(*refs, dates=dates),
        out_shape=(arr(LANES, n_slots), arr(planes, shard, n_slots)),
        in_specs=[VM],
        out_specs=(VM, VM),
        name="turn",
    )(*vmem(recv.reshape(n_slots, LANES)))
    coef = lax.all_to_all(share, "rhs", 0, 0).reshape(planes * shard, n_slots)

    comb = jnp.einsum("lcd,lde->lce", leaf_off, leaf_inv, precision=HI)
    comb_t = jnp.einsum("lcd,lde->lec", leaf_off, leaf_inv, precision=HI)
    rhs, update = pl.pallas_call(
        lambda *refs: forward_kernel(*refs, shard=shard),
        out_shape=(arr(local, dates, width), arr(local, dates, width)),
        in_specs=[VM, VM, VM],
        out_specs=(VM, VM),
        name="forward",
    )(*vmem(turned, coef, triple(comb_t)))
    both = lax.all_gather(update, "core", axis=0, tiled=True)

    places = q * (cores * local) + jnp.arange(cores * local, dtype=I32)
    held = leaf_map[None, :] == places[:, None]
    parent = jnp.sum(jnp.where(held, leaf_parent[None, :], 0), axis=1)
    parent = jnp.broadcast_to(parent[:, None], (cores * local, LANES))
    contrib = pl.pallas_call(
        reduce_kernel,
        out_shape=arr(half, dates, width),
        in_specs=[VM, VM],
        out_specs=VM,
        name="reduce",
    )(*vmem(both, parent))
    got = lax.all_to_all(contrib.reshape(chips, 1, pieces * width), "chip", 0, 0)

    p = c * half + q // span
    own_inv = lax.dynamic_index_in_dim(top_inv, p, 0, keepdims=False)
    gram = lax.dot_general(own_inv, own_inv, (((0,), (0,)), ((), ())), precision=HI)
    own_rhs = lax.dynamic_slice(top_rhs, (p, (q % span) * pieces, 0), (1, pieces, width))
    out = pl.pallas_call(
        middle_kernel,
        out_shape=arr(chips * pieces, width),
        in_specs=[VM, VM, VM],
        out_specs=VM,
        name="middle",
    )(*vmem(got.reshape(chips * pieces, width), own_rhs.reshape(pieces, width), triple(gram)))
    full = lax.all_to_all(out.reshape(chips, 1, pieces * width), "chip", 0, 0)
    full = lax.all_gather(full.reshape(half, dates, width), "core", axis=0, tiled=True)

    solved = jnp.einsum("ltc,ldc->ltd", rhs, leaf_inv, precision=HI)
    base = jnp.einsum("ltc,lcd->ltd", solved, leaf_inv, precision=HI)
    own_parent = lax.dynamic_slice_in_dim(parent, c * local, local, 0)
    return pl.pallas_call(
        last_kernel,
        out_shape=(
            jax.ShapeDtypeStruct((local, dates, width), F32),
            jax.ShapeDtypeStruct((tops, dates, width), F32),
        ),
        in_specs=[VM, VM, VM, VM],
        out_specs=(ANY, ANY),
        scratch_shapes=[
            pltpu.VMEM((local, dates, width), F32),
            pltpu.SemaphoreType.DMA((1 + local,)),
        ],
        name="last",
    )(*vmem(own_parent, full, base, triple(comb)))


def solution(mesh):
    devices = mesh.devices
    split = Mesh(devices.reshape(devices.shape[0] // 2, 2, -1), ("chip", "core", "rhs"))
    leaf = ("chip", "core")
    return jax.shard_map(
        body,
        mesh=split,
        in_specs=(
            P("rhs", leaf),
            P("rhs", leaf),
            P(leaf),
            P(),
            P(),
            P(leaf, None, None),
            P(leaf, None, None),
            P(),
            P(None, "rhs", None),
        ),
        out_specs=(P(leaf, "rhs", None), P(None, "rhs", None)),
        check_vma=False,
    )
```

time: 102 us -> 93.7 us (0.919)
  blocking collectives: 24 us -> 19.6 us
  Pallas kernels: 8.03 us -> 6.25 us
  local copies, waits for them, and re-layouts: 2.73 us -> 1.23 us
    all_gather x3 -> x1, blocking collectives: 13 us -> 8.46 us  [body(): pair = lax.all_gather(payload, 'core', axis=0)]
    pallas_call x1, Pallas kernels: 2.87 us -> 0.72 us  [body(): pl.pallas_call(lambda *refs: forward_kernel(*refs, shard=shard), out_shap...]
    all_to_all x1, waiting for transfers between devices: 10.3 us -> 11.4 us  [body(): lax.all_to_all(contrib.reshape(chips, 1, pieces * width), 'chip', 0, 0)]
    unnamed x12 -> x10, local copies, waits for them, and re-layouts: 1.44 us -> 0.31 us
    pallas_call x2 -> x4, Pallas kernels: 3.46 us -> 3.86 us  [the longest x1 1.14 us: body(): pl.pallas_call(lambda *refs: join_kernel(*refs, local=local, cores=cores)...]
  transfers between devices with their start and end apart: 4 -> 4, of which waited for: 4 -> 4; matrix products, arithmetic and copies ran while one was open for 3% -> 4% of each run, Pallas kernels for 0% -> 0%
where the time goes in v3:
time: 93.7 us; the launch traced here: 93.2 us
  waiting for transfers between devices  38.4 us (41%)
  starting transfers between devices  24.4 us (26%)
  blocking collectives  19.6 us (21%)
  Pallas kernels  6.25 us (7%)
  matrix products  2.28 us (2%)
  local copies, waits for them, and re-layouts  1.23 us (1%)
    all_to_all x1, waiting for transfers between devices, body(): recv = lax.all_to_all(placed.reshape(chips, slots, LANES), 'chip', 0, 0)  11.5 us
    all_to_all x1, waiting for transfers between devices, body(): lax.all_to_all(contrib.reshape(chips, 1, pieces * width), 'chip', 0, 0)  11.4 us
    all_to_all x1, starting transfers between devices, body(): recv = lax.all_to_all(placed.reshape(chips, slots, LANES), 'chip', 0, 0)  11.1 us
    all_to_all x1, waiting for transfers between devices, body(): full = lax.all_to_all(out.reshape(chips, 1, pieces * width), 'chip', 0, 0)  10.7 us
    all_gather x1, blocking collectives, body(): pair = lax.all_gather(payload, 'core', axis=0)  8.46 us
    all_gather x1, blocking collectives, body(): both = lax.all_gather(update, 'core', axis=0, tiled=True)  5.93 us
    all_gather x1, blocking collectives, body(): lax.all_gather(full.reshape(half, dates, width), 'core', axis=0, tiled=True)  5.16 us
    all_to_all x1, waiting for transfers between devices, body(): coef = lax.all_to_all(share, 'rhs', 0, 0).reshape(planes * shard, n_slots)  4.78 us
  transfers between devices with their start and end apart: 4, of which 4 were waited for; matrix products, arithmetic and copies ran while one was open for 4% of the time, Pallas kernels for 0%

profile of v3, /device:TPU:1, one launch (start us, length us, event | category | flops | bytes accessed | tf_op | source)
XLA Modules:
  0.0 93.2 jit_solution(11735295642295591679)
XLA Ops:
  0.6 0.0 copy-start
  0.6 1.1 %join.1 = f32[120,256]{1,0:T(8,128)S(1)} custom-call(s32[1,512]{1,0:T(1,128)} %bitcast.30, s32[1,256]{1,0:T(1,128)} %bitcast.31, f32[80,256]{1,0:T(8,128)} %refs_2_.1, f32[32,256]{1,0:T(8,128)} %refs_3_.1), custom_call_target="tpu_custom_call" | custom-call | tf_op jit(solution)/shard_map/join/pallas_call | solution.py:196
  1.8 8.5 %all-gather = f32[240,256]{1,0:T(8,128)S(1)} all-gather(f32[120,256]{1,0:T(8,128)S(1)} %join.1), channel_id=2, replica_groups=mesh['chip'=64,'core'=2,'rhs'=4] {'core'}, dimensions={0}, use_global_device_ids=true | all-gather | bytes 368640 | tf_op jit(solution)/shard_map/all_gather | solution.py:208
  10.3 1.0 %pack.1 = f32[512,128]{1,0:T(8,128)} custom-call(f32[2,120,256]{2,1,0:T(8,128)S(1)} %bitcast.27), custom_call_target="tpu_custom_call" | custom-call | tf_op jit(solution)/shard_map/pack/pallas_call | solution.py:209
  11.3 0.0 copy-start.3
  11.3 0.0 copy-start.4
  11.3 0.0 copy-start.2
  11.3 11.1 %all-to-all-start = ((f32[64,8,128]{2,1,0:T(8,128)}), f32[64,8,128]{2,1,0:T(8,128)S(1)}, u32[]{:S(2)}, u32[]{:S(2)}) async-start(f32[64,8,128]{2,1,0:T(8,128)} %bitcast.3), calls=%async_computation | async-start | bytes 524288 | tf_op jit(solution)/shard_map/all_to_all | solution.py:216
  22.4 0.0 copy-start.1
  22.4 0.0 copy-done.3
  22.4 0.0 copy-done.4
  22.4 0.2 select_reduce_fusion
  22.7 0.1 dynamic_slice.10
  22.7 0.0 copy-done
  22.7 0.3 reduce-precision_convert_fusion.2
  23.1 0.0 copy-done.2
  23.1 0.3 copy-done.1
  23.4 0.6 reduce-precision_convert_fusion.1
  24.0 11.5 %all-to-all-done = f32[64,8,128]{2,1,0:T(8,128)S(1)} async-done(((f32[64,8,128]{2,1,0:T(8,128)}), f32[64,8,128]{2,1,0:T(8,128)S(1)}, u32[]{:S(2)}, u32[]{:S(2)}) %all-to-all-start) | async-done | bytes 262176 | tf_op jit(solution)/shard_map/all_to_all | solution.py:216
  35.5 0.8 turn.1
  36.3 4.0 %all-to-all-start.1 = ((f32[4,32,512]{2,1,0:T(8,128)}), f32[4,32,512]{2,1,0:T(8,128)S(1)}, u32[]{:S(2)}, u32[]{:S(2)}) async-start(f32[4,32,512]{2,1,0:T(8,128)} %get-tuple-element.7), calls=%async_computation.1 | async-start | bytes 524288 | tf_op jit(solution)/shard_map/all_to_all | solution.py:224
  40.3 0.7 dynamic-slice_bitcast_fusion.rhs_ref
  41.1 4.8 %all-to-all-done.1 = f32[4,32,512]{2,1,0:T(8,128)S(1)} async-done(((f32[4,32,512]{2,1,0:T(8,128)}), f32[4,32,512]{2,1,0:T(8,128)S(1)}, u32[]{:S(2)}, u32[]{:S(2)}) %all-to-all-start.1) | async-done | bytes 262176 | tf_op jit(solution)/shard_map/all_to_all | solution.py:224
  45.9 0.7 forward.1
  46.6 5.9 %all_gather.14.both_ref = f32[8,80,128]{2,1,0:T(8,128)S(1)} all-gather(f32[4,80,128]{2,1,0:T(8,128)S(1)} %get-tuple-element.8), channel_id=1, replica_groups=mesh['chip'=64,'core'=2,'rhs'=4] {'core'}, dimensions={0}, use_global_device_ids=true | all-gather | bytes 491520 | tf_op jit(solution)/shard_map/all_gather | solution.py:235
  52.5 0.1 broadcast_in_dim.29.parent_ref
  52.6 0.8 reduce.1
  53.4 4.6 %all-to-all-start.2 = ((f32[64,1,640]{2,1,0:T(1,128)}), f32[64,1,640]{2,1,0:T(1,128)S(1)}, u32[]{:S(2)}, u32[]{:S(2)}) async-start(f32[64,1,640]{2,1,0:T(1,128)} %bitcast.6), calls=%async_computation.2 | async-start | bytes 327680 | tf_op jit(solution)/shard_map/all_to_all | solution.py:248
  58.0 0.4 reduce-precision_convert_fusion
  58.5 11.4 %all-to-all-done.2 = f32[64,1,640]{2,1,0:T(1,128)S(1)} async-done(((f32[64,1,640]{2,1,0:T(1,128)}), f32[64,1,640]{2,1,0:T(1,128)S(1)}, u32[]{:S(2)}, u32[]{:S(2)}) %all-to-all-start.2) | async-done | bytes 163872 | tf_op jit(solution)/shard_map/all_to_all | solution.py:248
  69.9 0.8 middle.1
  70.7 4.7 %all-to-all-start.3 = ((f32[64,1,640]{2,1,0:T(1,128)}), f32[64,1,640]{2,1,0:T(1,128)S(1)}, u32[]{:S(2)}, u32[]{:S(2)}) async-start(f32[64,1,640]{2,1,0:T(1,128)} %bitcast.10), calls=%async_computation.3 | async-start | bytes 327680 | tf_op jit(solution)/shard_map/all_to_all | solution.py:261
  75.4 0.6 fusion.7
  76.0 0.4 fusion.8.base_ref
  76.4 10.7 %all-to-all-done.3 = f32[64,1,640]{2,1,0:T(1,128)S(1)} async-done(((f32[64,1,640]{2,1,0:T(1,128)}), f32[64,1,640]{2,1,0:T(1,128)S(1)}, u32[]{:S(2)}, u32[]{:S(2)}) %all-to-all-start.3) | async-done | bytes 163872 | tf_op jit(solution)/shard_map/all_to_all | solution.py:261
  87.1 5.2 %all_gather.15.top_ref = f32[8,80,128]{2,1,0:T(8,128)S(1)} all-gather(f32[4,80,128]{2,1,0:T(8,128)S(1)} %bitcast.29), channel_id=1, replica_groups=mesh['chip'=64,'core'=2,'rhs'=4] {'core'}, dimensions={0}, use_global_device_ids=true | all-gather | bytes 491520 | tf_op jit(solution)/shard_map/all_gather | solution.py:262
  92.3 0.1 broadcast_in_dim.27.parent_ref
  92.3 0.9 last.1
  (4 shorter events, 0.1 us)
Async XLA Ops:
  0.6 22.1 %copy-start = (f32[8,128,128]{2,1,0:T(8,128)S(1)}, f32[8,128,128]{2,1,0:T(8,128)}, u32[]{:S(2)}) copy-start(f32[8,128,128]{2,1,0:T(8,128)} %param.16) | copy-start | bytes 1572868
  11.3 11.1 %copy-start.3 = (s32[512]{0:T(512)S(1)}, s32[512]{0:T(512)}, u32[]{:S(2)}) copy-start(s32[512]{0:T(512)} %param.12) | copy-start | bytes 6148
  11.3 11.1 %copy-start.4 = (s32[512]{0:T(512)S(1)}, s32[512]{0:T(512)}, u32[]{:S(2)}) copy-start(s32[512]{0:T(512)} %param.13) | copy-start | bytes 6148
  11.3 11.8 %copy-start.2 = (f32[4,128,128]{2,1,0:T(8,128)S(1)}, f32[4,128,128]{2,1,0:T(8,128)}, u32[]{:S(2)}) copy-start(f32[4,128,128]{2,1,0:T(8,128)} %param.15) | copy-start | bytes 786436
  11.3 24.2 %all-to-all-start = ((f32[64,8,128]{2,1,0:T(8,128)}), f32[64,8,128]{2,1,0:T(8,128)S(1)}, u32[]{:S(2)}, u32[]{:S(2)}) async-start(f32[64,8,128]{2,1,0:T(8,128)} %bitcast.3), calls=%async_computation | async-start | bytes 524288 | tf_op jit(solution)/shard_map/all_to_all | solution.py:216
  22.4 1.0 %copy-start.1 = (f32[4,128,128]{2,1,0:T(8,128)S(1)}, f32[4,128,128]{2,1,0:T(8,128)}, u32[]{:S(2)}) copy-start(f32[4,128,128]{2,1,0:T(8,128)} %param.14) | copy-start | bytes 786436
  36.3 9.5 %all-to-all-start.1 = ((f32[4,32,512]{2,1,0:T(8,128)}), f32[4,32,512]{2,1,0:T(8,128)S(1)}, u32[]{:S(2)}, u32[]{:S(2)}) async-start(f32[4,32,512]{2,1,0:T(8,128)} %get-tuple-element.7), calls=%async_computation.1 | async-start | bytes 524288 | tf_op jit(solution)/shard_map/all_to_all | solution.py:224
  53.4 16.5 %all-to-all-start.2 = ((f32[64,1,640]{2,1,0:T(1,128)}), f32[64,1,640]{2,1,0:T(1,128)S(1)}, u32[]{:S(2)}, u32[]{:S(2)}) async-start(f32[64,1,640]{2,1,0:T(1,128)} %bitcast.6), calls=%async_computation.2 | async-start | bytes 327680 | tf_op jit(solution)/shard_map/all_to_all | solution.py:248
  70.7 16.4 %all-to-all-start.3 = ((f32[64,1,640]{2,1,0:T(1,128)}), f32[64,1,640]{2,1,0:T(1,128)S(1)}, u32[]{:S(2)}, u32[]{:S(2)}) async-start(f32[64,1,640]{2,1,0:T(1,128)} %bitcast.10), calls=%async_computation.3 | async-start | bytes 327680 | tf_op jit(solution)/shard_map/all_to_all | solution.py:261

commit v4 on v3

--- a/solution.py
+++ b/solution.py
@@ -1,3 +1,5 @@
+import math
+
 import jax
 import jax.numpy as jnp
 from jax import lax
@@ -11,6 +13,16 @@
 NT = (((1,), (1,)), ((), ()))
 NN = (((1,), (0,)), ((), ()))
 F32, BF16, I32 = jnp.float32, jnp.bfloat16, jnp.int32
+
+
+def far_index(count):
+    side = math.isqrt(count)
+    return side // 2 * side + side // 2
+
+
+def exchange(x, axis, far):
+    order = [i ^ far for i in range(x.shape[0])]
+    return lax.all_to_all(x, axis, 0, 0, axis_index_groups=[order])
 
 
 def split2(x):
@@ -54,7 +66,7 @@
     owner = found[0:1, :].astype(I32)
     same = (owner_ids == owner).astype(F32)
     rank = jnp.sum(same * dot(same.astype(BF16), before, NN), axis=0, keepdims=True)
-    slot = (owner // cores) * (cores * CAP) + rank.astype(I32)
+    slot = ((owner // cores) ^ far_index(chips)) * (cores * CAP) + rank.astype(I32)
     code = (owner % cores) * (chips * cores * CAP) + slot + lax.axis_index("core") * CAP
     tail = out_ref.shape[0] - dates - shard
     out_ref[dates + shard :, :] = jnp.concatenate(
@@ -89,7 +101,9 @@
     local, dates, _ = rhs_ref.shape
     data = turned_ref[0:dates, :]
     mark = turned_ref[dates + shard : dates + shard + 1, :]
-    coef_high, coef_low = split2(coef_ref[...])
+    planes = coef_ref.shape[0]
+    order = [coef_ref[i ^ (planes // 2)] for i in range(planes)]
+    coef_high, coef_low = split2(jnp.concatenate(order, axis=0))
     coef = jnp.concatenate([coef_high, coef_high, coef_low], axis=1)
     picked = jnp.concatenate(
         [jnp.where(mark == float(k + 1), data, 0.0) for k in range(local)], axis=0
@@ -192,6 +206,7 @@
     pieces = half * dates // chips
     span = dates // pieces
     height = dates + shard + 8
+    far = far_index(chips)
 
     payload = pl.pallas_call(
         lambda *refs: join_kernel(*refs, local=local, cores=cores),
@@ -213,7 +228,7 @@
         out_specs=VM,
         name="pack",
     )(*vmem(pair))
-    recv = lax.all_to_all(placed.reshape(chips, slots, LANES), "chip", 0, 0)
+    recv = exchange(placed.reshape(chips, slots, LANES), "chip", far)
     turned, share = pl.pallas_call(
         lambda *refs: turn_kernel(*refs, dates=dates),
         out_shape=(arr(LANES, n_slots), arr(planes, shard, n_slots)),
@@ -221,7 +236,7 @@
         out_specs=(VM, VM),
         name="turn",
     )(*vmem(recv.reshape(n_slots, LANES)))
-    coef = lax.all_to_all(share, "rhs", 0, 0).reshape(planes * shard, n_slots)
+    coef = exchange(share, "rhs", planes // 2)
 
     comb = jnp.einsum("lcd,lde->lce", leaf_off, leaf_inv, precision=HI)
     comb_t = jnp.einsum("lcd,lde->lec", leaf_off, leaf_inv, precision=HI)
@@ -245,12 +260,13 @@
         out_specs=VM,
         name="reduce",
     )(*vmem(both, parent))
-    got = lax.all_to_all(contrib.reshape(chips, 1, pieces * width), "chip", 0, 0)
-
-    p = c * half + q // span
+    got = exchange(contrib.reshape(chips, 1, pieces * width), "chip", far)
+
+    piece = q ^ far
+    p = c * half + piece // span
     own_inv = lax.dynamic_index_in_dim(top_inv, p, 0, keepdims=False)
     gram = lax.dot_general(own_inv, own_inv, (((0,), (0,)), ((), ())), precision=HI)
-    own_rhs = lax.dynamic_slice(top_rhs, (p, (q % span) * pieces, 0), (1, pieces, width))
+    own_rhs = lax.dynamic_slice(top_rhs, (p, (piece % span) * pieces, 0), (1, pieces, width))
     out = pl.pallas_call(
         middle_kernel,
         out_shape=arr(chips * pieces, width),
@@ -258,7 +274,7 @@
         out_specs=VM,
         name="middle",
     )(*vmem(got.reshape(chips * pieces, width), own_rhs.reshape(pieces, width), triple(gram)))
-    full = lax.all_to_all(out.reshape(chips, 1, pieces * width), "chip", 0, 0)
+    full = exchange(out.reshape(chips, 1, pieces * width), "chip", far)
     full = lax.all_gather(full.reshape(half, dates, width), "core", axis=0, tiled=True)
 
     solved = jnp.einsum("ltc,ldc->ltd", rhs, leaf_inv, precision=HI)

time: 93.7 us -> 86.9 us (0.927)
  waiting for transfers between devices: 38.4 us -> 12.8 us
  starting transfers between devices: 24.4 us -> 45.6 us
  blocking collectives: 19.6 us -> 17.1 us
    all_to_all x4, waiting for transfers between devices: 38.4 us -> 12.8 us  [exchange(): return lax.all_to_all(x, axis, 0, 0, axis_index_groups=[order])]
    all_to_all x4, starting transfers between devices: 24.4 us -> 45.6 us  [exchange(): return lax.all_to_all(x, axis, 0, 0, axis_index_groups=[order])]
    all_gather x1, blocking collectives: 5.93 us -> 3.88 us  [body(): both = lax.all_gather(update, 'core', axis=0, tiled=True)]
where the time goes in v4:
time: 86.9 us; the launch traced here: 86.4 us
  starting transfers between devices  45.6 us (52%)
  blocking collectives  17.1 us (20%)
  waiting for transfers between devices  12.8 us (15%)
  Pallas kernels  6.25 us (7%)
  matrix products  2.28 us (3%)
  local copies, waits for them, and re-layouts  1.22 us (1%)
    all_to_all x4, starting transfers between devices, exchange(): return lax.all_to_all(x, axis, 0, 0, axis_index_groups=[order])  45.6 us
    all_to_all x4, waiting for transfers between devices, exchange(): return lax.all_to_all(x, axis, 0, 0, axis_index_groups=[order])  12.8 us
    all_gather x1, blocking collectives, body(): pair = lax.all_gather(payload, 'core', axis=0)  8.46 us
    all_gather x1, blocking collectives, body(): lax.all_gather(full.reshape(half, dates, width), 'core', axis=0, tiled=True)  4.8 us
    all_gather x1, blocking collectives, body(): both = lax.all_gather(update, 'core', axis=0, tiled=True)  3.88 us
  transfers between devices with their start and end apart: 4, of which 4 were waited for; matrix products, arithmetic and copies ran while one was open for 4% of the time, Pallas kernels for 0%

profile of v4, /device:TPU:1, one launch (start us, length us, event | category | flops | bytes accessed | tf_op | source)
XLA Modules:
  0.0 86.4 jit_solution(1424383635008406336)
XLA Ops:
  0.6 0.0 copy-start
  0.6 1.1 %join.1 = f32[120,256]{1,0:T(8,128)S(1)} custom-call(s32[1,512]{1,0:T(1,128)} %bitcast.28, s32[1,256]{1,0:T(1,128)} %bitcast.29, f32[80,256]{1,0:T(8,128)} %refs_2_.1, f32[32,256]{1,0:T(8,128)} %refs_3_.1), custom_call_target="tpu_custom_call" | custom-call | tf_op jit(solution)/shard_map/join/pallas_call | solution.py:211
  1.8 8.5 %all-gather = f32[240,256]{1,0:T(8,128)S(1)} all-gather(f32[120,256]{1,0:T(8,128)S(1)} %join.1), channel_id=2, replica_groups=mesh['chip'=64,'core'=2,'rhs'=4] {'core'}, dimensions={0}, use_global_device_ids=true | all-gather | bytes 368640 | tf_op jit(solution)/shard_map/all_gather | solution.py:223
  10.3 1.0 %pack.1 = f32[512,128]{1,0:T(8,128)} custom-call(f32[2,120,256]{2,1,0:T(8,128)S(1)} %bitcast.25), custom_call_target="tpu_custom_call" | custom-call | tf_op jit(solution)/shard_map/pack/pallas_call | solution.py:224
  11.3 0.0 copy-start.3
  11.3 0.0 copy-start.4
  11.3 0.0 copy-start.2
  11.3 14.1 %all-to-all-start = ((f32[64,8,128]{2,1,0:T(8,128)}), f32[64,8,128]{2,1,0:T(8,128)S(1)}, u32[]{:S(2)}, u32[]{:S(2)}) async-start(f32[64,8,128]{2,1,0:T(8,128)} %bitcast.3), calls=%async_computation | async-start | bytes 524288 | tf_op jit(solution)/shard_map/all_to_all | solution.py:25
  25.4 0.0 copy-start.1
  25.4 0.0 copy-done.3
  25.4 0.0 copy-done.4
  25.4 0.2 select_reduce_fusion
  25.7 0.1 dynamic_slice.10
  25.7 0.0 copy-done
  25.7 0.3 reduce-precision_convert_fusion.2
  26.1 0.0 copy-done.2
  26.1 0.3 copy-done.1
  26.3 0.6 reduce-precision_convert_fusion.1
  27.0 4.8 %all-to-all-done = f32[64,8,128]{2,1,0:T(8,128)S(1)} async-done(((f32[64,8,128]{2,1,0:T(8,128)}), f32[64,8,128]{2,1,0:T(8,128)S(1)}, u32[]{:S(2)}, u32[]{:S(2)}) %all-to-all-start) | async-done | bytes 262176 | tf_op jit(solution)/shard_map/all_to_all | solution.py:25
  31.8 0.8 turn.1
  32.6 6.1 %all-to-all-start.1 = ((f32[4,32,512]{2,1,0:T(8,128)}), f32[4,32,512]{2,1,0:T(8,128)S(1)}, u32[]{:S(2)}, u32[]{:S(2)}) async-start(f32[4,32,512]{2,1,0:T(8,128)} %get-tuple-element.7), calls=%async_computation.1 | async-start | bytes 524288 | tf_op jit(solution)/shard_map/all_to_all | solution.py:25
  38.7 0.7 dynamic-slice_bitcast_fusion.rhs_ref
  39.5 2.1 %all-to-all-done.1.refs_1_ = f32[4,32,512]{2,1,0:T(8,128)S(1)} async-done(((f32[4,32,512]{2,1,0:T(8,128)}), f32[4,32,512]{2,1,0:T(8,128)S(1)}, u32[]{:S(2)}, u32[]{:S(2)}) %all-to-all-start.1) | async-done | bytes 262176 | tf_op jit(solution)/shard_map/all_to_all | solution.py:25
  41.6 0.7 forward.1
  42.3 3.9 %all_gather.14.both_ref = f32[8,80,128]{2,1,0:T(8,128)S(1)} all-gather(f32[4,80,128]{2,1,0:T(8,128)S(1)} %get-tuple-element.8), channel_id=1, replica_groups=mesh['chip'=64,'core'=2,'rhs'=4] {'core'}, dimensions={0}, use_global_device_ids=true | all-gather | bytes 491520 | tf_op jit(solution)/shard_map/all_gather | solution.py:250
  46.2 0.1 broadcast_in_dim.29.parent_ref
  46.3 0.8 reduce.1
  47.0 13.1 %all-to-all-start.2 = ((f32[64,1,640]{2,1,0:T(1,128)}), f32[64,1,640]{2,1,0:T(1,128)S(1)}, u32[]{:S(2)}, u32[]{:S(2)}) async-start(f32[64,1,640]{2,1,0:T(1,128)} %bitcast.5), calls=%async_computation.2 | async-start | bytes 327680 | tf_op jit(solution)/shard_map/all_to_all | solution.py:25
  60.1 0.4 reduce-precision_convert_fusion
  60.6 3.8 %all-to-all-done.2 = f32[64,1,640]{2,1,0:T(1,128)S(1)} async-done(((f32[64,1,640]{2,1,0:T(1,128)}), f32[64,1,640]{2,1,0:T(1,128)S(1)}, u32[]{:S(2)}, u32[]{:S(2)}) %all-to-all-start.2) | async-done | bytes 163872 | tf_op jit(solution)/shard_map/all_to_all | solution.py:25
  64.4 0.8 middle.1
  65.2 12.3 %all-to-all-start.3 = ((f32[64,1,640]{2,1,0:T(1,128)}), f32[64,1,640]{2,1,0:T(1,128)S(1)}, u32[]{:S(2)}, u32[]{:S(2)}) async-start(f32[64,1,640]{2,1,0:T(1,128)} %bitcast.9), calls=%async_computation.3 | async-start | bytes 327680 | tf_op jit(solution)/shard_map/all_to_all | solution.py:25
  77.5 0.6 fusion.7
  78.1 0.4 fusion.8.base_ref
  78.5 2.1 %all-to-all-done.3 = f32[64,1,640]{2,1,0:T(1,128)S(1)} async-done(((f32[64,1,640]{2,1,0:T(1,128)}), f32[64,1,640]{2,1,0:T(1,128)S(1)}, u32[]{:S(2)}, u32[]{:S(2)}) %all-to-all-start.3) | async-done | bytes 163872 | tf_op jit(solution)/shard_map/all_to_all | solution.py:25
  80.6 4.8 %all_gather.15.top_ref = f32[8,80,128]{2,1,0:T(8,128)S(1)} all-gather(f32[4,80,128]{2,1,0:T(8,128)S(1)} %bitcast.27), channel_id=1, replica_groups=mesh['chip'=64,'core'=2,'rhs'=4] {'core'}, dimensions={0}, use_global_device_ids=true | all-gather | bytes 491520 | tf_op jit(solution)/shard_map/all_gather | solution.py:278
  85.4 0.1 broadcast_in_dim.27.parent_ref
  85.5 0.9 %last.1 = (f32[4,80,128]{2,1,0:T(8,128)}, f32[8,80,128]{2,1,0:T(8,128)}) custom-call(s32[4,128]{1,0:T(4,128)S(1)} %broadcast_in_dim.27.parent_ref, f32[8,80,128]{2,1,0:T(8,128)S(1)} %all_gather.15.top_ref, f32[4,80,128]{2,1,0:T(8,128)S(1)} %fusion.8.base_ref, bf16[4,384,128]{2,1,0:T(8,128)(2,1)S(1)} %pad_maximum_fusion.1.comb_ref), custom_call_target="tpu_custom_call" | custom-call | tf_op jit(solution)/shard_map/last/pallas_call | solution.py:283
  (4 shorter events, 0.1 us)
Async XLA Ops:
  0.6 25.1 %copy-start = (f32[8,128,128]{2,1,0:T(8,128)S(1)}, f32[8,128,128]{2,1,0:T(8,128)}, u32[]{:S(2)}) copy-start(f32[8,128,128]{2,1,0:T(8,128)} %param.16) | copy-start | bytes 1572868
  11.3 14.1 %copy-start.3 = (s32[512]{0:T(512)S(1)}, s32[512]{0:T(512)}, u32[]{:S(2)}) copy-start(s32[512]{0:T(512)} %param.12) | copy-start | bytes 6148
  11.3 14.1 %copy-start.4 = (s32[512]{0:T(512)S(1)}, s32[512]{0:T(512)}, u32[]{:S(2)}) copy-start(s32[512]{0:T(512)} %param.13) | copy-start | bytes 6148
  11.3 14.8 %copy-start.2 = (f32[4,128,128]{2,1,0:T(8,128)S(1)}, f32[4,128,128]{2,1,0:T(8,128)}, u32[]{:S(2)}) copy-start(f32[4,128,128]{2,1,0:T(8,128)} %param.15) | copy-start | bytes 786436
  11.3 20.5 %all-to-all-start = ((f32[64,8,128]{2,1,0:T(8,128)}), f32[64,8,128]{2,1,0:T(8,128)S(1)}, u32[]{:S(2)}, u32[]{:S(2)}) async-start(f32[64,8,128]{2,1,0:T(8,128)} %bitcast.3), calls=%async_computation | async-start | bytes 524288 | tf_op jit(solution)/shard_map/all_to_all | solution.py:25
  25.4 1.0 %copy-start.1 = (f32[4,128,128]{2,1,0:T(8,128)S(1)}, f32[4,128,128]{2,1,0:T(8,128)}, u32[]{:S(2)}) copy-start(f32[4,128,128]{2,1,0:T(8,128)} %param.14) | copy-start | bytes 786436
  32.6 9.0 %all-to-all-start.1 = ((f32[4,32,512]{2,1,0:T(8,128)}), f32[4,32,512]{2,1,0:T(8,128)S(1)}, u32[]{:S(2)}, u32[]{:S(2)}) async-start(f32[4,32,512]{2,1,0:T(8,128)} %get-tuple-element.7), calls=%async_computation.1 | async-start | bytes 524288 | tf_op jit(solution)/shard_map/all_to_all | solution.py:25
  47.0 17.3 %all-to-all-start.2 = ((f32[64,1,640]{2,1,0:T(1,128)}), f32[64,1,640]{2,1,0:T(1,128)S(1)}, u32[]{:S(2)}, u32[]{:S(2)}) async-start(f32[64,1,640]{2,1,0:T(1,128)} %bitcast.5), calls=%async_computation.2 | async-start | bytes 327680 | tf_op jit(solution)/shard_map/all_to_all | solution.py:25
  65.2 15.4 %all-to-all-start.3 = ((f32[64,1,640]{2,1,0:T(1,128)}), f32[64,1,640]{2,1,0:T(1,128)S(1)}, u32[]{:S(2)}, u32[]{:S(2)}) async-start(f32[64,1,640]{2,1,0:T(1,128)} %bitcast.9), calls=%async_computation.3 | async-start | bytes 327680 | tf_op jit(solution)/shard_map/all_to_all | solution.py:25

commit v5 on v4

--- a/solution.py
+++ b/solution.py
@@ -97,8 +97,8 @@
         share_ref[i] = turned[dates : dates + shard, :]
 
 
-def forward_kernel(turned_ref, coef_ref, comb_ref, rhs_ref, update_ref, *, shard):
-    local, dates, _ = rhs_ref.shape
+def forward_kernel(turned_ref, coef_ref, comb_ref, rows_ref, update_ref, *, shard):
+    local, dates, _ = update_ref.shape
     data = turned_ref[0:dates, :]
     mark = turned_ref[dates + shard : dates + shard + 1, :]
     planes = coef_ref.shape[0]
@@ -112,10 +112,9 @@
     rhs = dot(jnp.concatenate([high, low, high], axis=1), coef, NT)
     high, low = split2(rhs)
     rows = jnp.concatenate([high, low, high], axis=1)
+    rows_ref[...] = rows
     for k in range(local):
-        part = slice(k * dates, (k + 1) * dates)
-        rhs_ref[k] = rhs[part]
-        update_ref[k] = dot(rows[part], comb_ref[k], NN)
+        update_ref[k] = dot(rows[k * dates : (k + 1) * dates], comb_ref[k], NN)
 
 
 def reduce_kernel(both_ref, parent_ref, out_ref):
@@ -146,8 +145,8 @@
         )
 
 
-def last_kernel(parent_ref, top_ref, base_ref, comb_ref, out_hbm, top_hbm, out_ref, sems):
-    local = out_ref.shape[0]
+def last_kernel(parent_ref, top_ref, rows_ref, both_ref, out_hbm, top_hbm, out_ref, sems):
+    local, dates, _ = out_ref.shape
     tops = top_ref.shape[0]
     copy_top = pltpu.make_async_copy(top_ref, top_hbm, sems.at[0])
     copy_top.start()
@@ -158,8 +157,8 @@
         for p in range(1, tops):
             x = jnp.where(parent == p, top_ref[p], x)
         high, low = split2(x)
-        lifted = dot(jnp.concatenate([high, low, high], axis=1), comb_ref[k], NN)
-        out_ref[k] = base_ref[k] - lifted
+        rows = rows_ref[k * dates : (k + 1) * dates, :]
+        out_ref[k] = dot(jnp.concatenate([rows, high, low, high], axis=1), both_ref[k], NN)
         copies.append(pltpu.make_async_copy(out_ref.at[k], out_hbm.at[k], sems.at[1 + k]))
         copies[-1].start()
     copy_top.wait()
@@ -229,6 +228,27 @@
         name="pack",
     )(*vmem(pair))
     recv = exchange(placed.reshape(chips, slots, LANES), "chip", far)
+
+    update_by = triple(jnp.einsum("lcd,lde->lec", leaf_off, leaf_inv, precision=HI))
+    product = jnp.einsum("lcd,lde->lce", leaf_off, leaf_inv, precision=HI)
+    square = jnp.einsum("ldc,lde->lce", leaf_inv, leaf_inv, precision=HI)
+    solve_by = jnp.concatenate([triple(square), triple(-product)], axis=1)
+    places = q * (cores * local) + jnp.arange(cores * local, dtype=I32)
+    held = leaf_map[None, :] == places[:, None]
+    parent = jnp.sum(jnp.where(held, leaf_parent[None, :], 0), axis=1)
+    own_parent = lax.dynamic_slice_in_dim(parent, c * local, local, 0)
+    parent = jnp.broadcast_to(parent[:, None], (cores * local, LANES))
+    own_parent = jnp.broadcast_to(own_parent[:, None], (local, LANES))
+    piece = q ^ far
+    p = c * half + piece // span
+    own_inv = lax.dynamic_index_in_dim(top_inv, p, 0, keepdims=False)
+    gram = triple(lax.dot_general(own_inv, own_inv, (((0,), (0,)), ((), ())), precision=HI))
+    own_rhs = lax.dynamic_slice(top_rhs, (p, (piece % span) * pieces, 0), (1, pieces, width))
+    own_rhs = own_rhs.reshape(pieces, width)
+    recv, update_by, solve_by, parent, own_parent, gram, own_rhs = lax.optimization_barrier(
+        (recv, update_by, solve_by, parent, own_parent, gram, own_rhs)
+    )
+
     turned, share = pl.pallas_call(
         lambda *refs: turn_kernel(*refs, dates=dates),
         out_shape=(arr(LANES, n_slots), arr(planes, shard, n_slots)),
@@ -237,22 +257,14 @@
         name="turn",
     )(*vmem(recv.reshape(n_slots, LANES)))
     coef = exchange(share, "rhs", planes // 2)
-
-    comb = jnp.einsum("lcd,lde->lce", leaf_off, leaf_inv, precision=HI)
-    comb_t = jnp.einsum("lcd,lde->lec", leaf_off, leaf_inv, precision=HI)
-    rhs, update = pl.pallas_call(
+    parts, update = pl.pallas_call(
         lambda *refs: forward_kernel(*refs, shard=shard),
-        out_shape=(arr(local, dates, width), arr(local, dates, width)),
+        out_shape=(pltpu.VMEM((local * dates, 3 * width), BF16), arr(local, dates, width)),
         in_specs=[VM, VM, VM],
         out_specs=(VM, VM),
         name="forward",
-    )(*vmem(turned, coef, triple(comb_t)))
+    )(*vmem(turned, coef, update_by))
     both = lax.all_gather(update, "core", axis=0, tiled=True)
-
-    places = q * (cores * local) + jnp.arange(cores * local, dtype=I32)
-    held = leaf_map[None, :] == places[:, None]
-    parent = jnp.sum(jnp.where(held, leaf_parent[None, :], 0), axis=1)
-    parent = jnp.broadcast_to(parent[:, None], (cores * local, LANES))
     contrib = pl.pallas_call(
         reduce_kernel,
         out_shape=arr(half, dates, width),
@@ -261,25 +273,15 @@
         name="reduce",
     )(*vmem(both, parent))
     got = exchange(contrib.reshape(chips, 1, pieces * width), "chip", far)
-
-    piece = q ^ far
-    p = c * half + piece // span
-    own_inv = lax.dynamic_index_in_dim(top_inv, p, 0, keepdims=False)
-    gram = lax.dot_general(own_inv, own_inv, (((0,), (0,)), ((), ())), precision=HI)
-    own_rhs = lax.dynamic_slice(top_rhs, (p, (piece % span) * pieces, 0), (1, pieces, width))
     out = pl.pallas_call(
         middle_kernel,
         out_shape=arr(chips * pieces, width),
         in_specs=[VM, VM, VM],
         out_specs=VM,
         name="middle",
-    )(*vmem(got.reshape(chips * pieces, width), own_rhs.reshape(pieces, width), triple(gram)))
+    )(*vmem(got.reshape(chips * pieces, width), own_rhs, gram))
     full = exchange(out.reshape(chips, 1, pieces * width), "chip", far)
     full = lax.all_gather(full.reshape(half, dates, width), "core", axis=0, tiled=True)
-
-    solved = jnp.einsum("ltc,ldc->ltd", rhs, leaf_inv, precision=HI)
-    base = jnp.einsum("ltc,lcd->ltd", solved, leaf_inv, precision=HI)
-    own_parent = lax.dynamic_slice_in_dim(parent, c * local, local, 0)
     return pl.pallas_call(
         last_kernel,
         out_shape=(
@@ -293,7 +295,7 @@
             pltpu.SemaphoreType.DMA((1 + local,)),
         ],
         name="last",
-    )(*vmem(own_parent, full, base, triple(comb)))
+    )(*vmem(own_parent, full, parts, solve_by))
 
 
 def solution(mesh):

time: 86.9 us -> 82 us (0.944)
  blocking collectives: 17.1 us -> 56 us
  starting transfers between devices: 45.6 us -> 14.1 us
  waiting for transfers between devices: 12.8 us -> 1.56 us
  Pallas kernels: 6.25 us -> 4.27 us
  local copies, waits for them, and re-layouts: 1.22 us -> 2.51 us
    all_to_all x0 -> x3, blocking collectives: none -> 39.8 us  [exchange(): return lax.all_to_all(x, axis, 0, 0, axis_index_groups=[order])]
    all_to_all x4 -> x1, starting transfers between devices: 45.6 us -> 14.1 us  [exchange(): return lax.all_to_all(x, axis, 0, 0, axis_index_groups=[order])]
    all_to_all x4 -> x1, waiting for transfers between devices: 12.8 us -> 1.56 us  [exchange(): return lax.all_to_all(x, axis, 0, 0, axis_index_groups=[order])]
    unnamed x10, local copies, waits for them, and re-layouts: 0.3 us -> 1.58 us
    dot_general x4 -> x3, matrix products: 2 us -> 1.62 us  [the longest x1 0.6 us: body(): jnp.einsum('lcd,lde->lec', leaf_off, leaf_inv, precision=HI)]
  transfers between devices with their start and end apart: 4 -> 1, of which waited for: 4 -> 1; matrix products, arithmetic and copies ran while one was open for 4% -> 4% of each run, Pallas kernels for 0% -> 0%
where the time goes in v5:
time: 82 us; the launch traced here: 81.6 us
  blocking collectives  56 us (68%)
  starting transfers between devices  14.1 us (17%)
  Pallas kernels  4.27 us (5%)
  local copies, waits for them, and re-layouts  2.51 us (3%)
  matrix products  1.91 us (2%)
  waiting for transfers between devices  1.56 us (2%)
  between operations  0.84 us (1%)
    all_to_all x3, blocking collectives, exchange(): return lax.all_to_all(x, axis, 0, 0, axis_index_groups=[order])  39.8 us
    all_to_all x1, starting transfers between devices, exchange(): return lax.all_to_all(x, axis, 0, 0, axis_index_groups=[order])  14.1 us
    all_gather x1, blocking collectives, body(): pair = lax.all_gather(payload, 'core', axis=0)  8.46 us
    all_gather x1, blocking collectives, body(): lax.all_gather(full.reshape(half, dates, width), 'core', axis=0, tiled=True)  4.26 us
    all_gather x1, blocking collectives, body(): both = lax.all_gather(update, 'core', axis=0, tiled=True)  3.56 us
  transfers between devices with their start and end apart: 1, of which 1 were waited for; matrix products, arithmetic and copies ran while one was open for 4% of the time, Pallas kernels for 0%

profile of v5, /device:TPU:1, one launch (start us, length us, event | category | flops | bytes accessed | tf_op | source)
XLA Modules:
  0.0 81.6 jit_solution(15602324159886331386)
XLA Ops:
  0.6 0.0 copy-start
  0.6 1.1 %join.1 = f32[120,256]{1,0:T(8,128)S(1)} custom-call(s32[1,512]{1,0:T(1,128)} %bitcast.28, s32[1,256]{1,0:T(1,128)} %bitcast.29, f32[80,256]{1,0:T(8,128)} %refs_2_.1, f32[32,256]{1,0:T(8,128)} %refs_3_.1), custom_call_target="tpu_custom_call" | custom-call | tf_op jit(solution)/shard_map/join/pallas_call | solution.py:210
  1.8 8.5 %all-gather = f32[240,256]{1,0:T(8,128)S(1)} all-gather(f32[120,256]{1,0:T(8,128)S(1)} %join.1), channel_id=2, replica_groups=mesh['chip'=64,'core'=2,'rhs'=4] {'core'}, dimensions={0}, use_global_device_ids=true | all-gather | bytes 368640 | tf_op jit(solution)/shard_map/all_gather | solution.py:222
  10.3 1.0 %pack.1 = f32[512,128]{1,0:T(8,128)} custom-call(f32[2,120,256]{2,1,0:T(8,128)S(1)} %bitcast.23), custom_call_target="tpu_custom_call" | custom-call | tf_op jit(solution)/shard_map/pack/pallas_call | solution.py:223
  11.3 0.0 copy-start.1
  11.3 14.1 %all-to-all-start = ((f32[64,8,128]{2,1,0:T(8,128)}), f32[64,8,128]{2,1,0:T(8,128)S(1)}, u32[]{:S(2)}, u32[]{:S(2)}) async-start(f32[64,8,128]{2,1,0:T(8,128)} %bitcast.3), calls=%async_computation | async-start | bytes 524288 | tf_op jit(solution)/shard_map/all_to_all | solution.py:25
  25.4 0.0 copy-done.1
  25.4 0.6 fusion.9
  26.1 0.0 copy-start.2
  26.1 0.1 fusion.4
  26.1 0.9 %copy-done.2 = f32[4,128,128]{2,1,0:T(8,128)S(1)} copy-done((f32[4,128,128]{2,1,0:T(8,128)S(1)}, f32[4,128,128]{2,1,0:T(8,128)}, u32[]{:S(2)}) %copy-start.2) | copy-done | bytes 262168
  27.0 0.6 reduce-precision_convert_fusion.2
  27.6 0.4 fusion.11
  28.1 0.0 copy-done
  28.1 0.3 reduce-precision_convert_fusion.3
  28.4 0.0 copy-start.4
  28.4 0.0 copy-start.3
  28.4 0.6 copy-done.4
  29.1 0.0 copy-done.3
  29.1 0.2 select_reduce_fusion
  29.3 0.7 dynamic-slice_bitcast_fusion.rhs_ref
  30.1 0.1 dynamic_slice.10
  30.2 0.1 fusion.3.both_ref
  30.2 1.6 %all-to-all-done = f32[64,8,128]{2,1,0:T(8,128)S(1)} async-done(((f32[64,8,128]{2,1,0:T(8,128)}), f32[64,8,128]{2,1,0:T(8,128)S(1)}, u32[]{:S(2)}, u32[]{:S(2)}) %all-to-all-start) | async-done | bytes 262176 | tf_op jit(solution)/shard_map/all_to_all | solution.py:25
  31.8 0.1 broadcast_in_dim.30.parent_ref
  31.8 0.1 broadcast_in_dim.18.parent_ref
  31.9 0.1 turn.1
  32.1 8.3 %all_to_all.20.refs_1_ = f32[4,32,512]{2,1,0:T(8,128)S(1)} all-to-all(f32[4,32,512]{2,1,0:T(8,128)S(1)} %get-tuple-element.16), channel_id=1, replica_groups={{2,3,0,1},{6,7,4,5},{10,11,8,9},{14,15,12,13},{18,19,16,17},{22,23,20,2..., dimensions={0} | all-to-all | bytes 524288 | tf_op jit(solution)/shard_map/all_to_all | solution.py:25
  40.3 0.7 forward.1
  41.0 3.6 %all_gather.14.both_ref = f32[8,80,128]{2,1,0:T(8,128)S(1)} all-gather(f32[4,80,128]{2,1,0:T(8,128)S(1)} %get-tuple-element.18), channel_id=1, replica_groups=mesh['chip'=64,'core'=2,'rhs'=4] {'core'}, dimensions={0}, use_global_device_ids=true | all-gather | bytes 491520 | tf_op jit(solution)/shard_map/all_gather | solution.py:267
  44.6 0.1 reduce.1
  44.7 16.2 %all_to_all.21 = f32[64,1,640]{2,1,0:T(1,128)S(1)} all-to-all(f32[64,1,640]{2,1,0:T(1,128)S(1)} %bitcast.26), channel_id=1, replica_groups={{288,296,304,312,256,264,272,280,352,360,368,376,320,328,336,344,416,42..., dimensions={0} | all-to-all | bytes 327680 | tf_op jit(solution)/shard_map/all_to_all | solution.py:25
  61.0 0.2 middle.1
  61.1 15.3 %all_to_all.22 = f32[64,1,640]{2,1,0:T(1,128)S(1)} all-to-all(f32[64,1,640]{2,1,0:T(1,128)S(1)} %bitcast.25), channel_id=1, replica_groups={{288,296,304,312,256,264,272,280,352,360,368,376,320,328,336,344,416,42..., dimensions={0} | all-to-all | bytes 327680 | tf_op jit(solution)/shard_map/all_to_all | solution.py:25
  76.4 4.3 %all_gather.15.top_ref = f32[8,80,128]{2,1,0:T(8,128)S(1)} all-gather(f32[4,80,128]{2,1,0:T(8,128)S(1)} %bitcast.27), channel_id=1, replica_groups=mesh['chip'=64,'core'=2,'rhs'=4] {'core'}, dimensions={0}, use_global_device_ids=true | all-gather | bytes 491520 | tf_op jit(solution)/shard_map/all_gather | solution.py:284
  80.6 1.0 %last.1 = (f32[4,80,128]{2,1,0:T(8,128)}, f32[8,80,128]{2,1,0:T(8,128)}) custom-call(s32[4,128]{1,0:T(4,128)S(1)} %broadcast_in_dim.30.parent_ref, f32[8,80,128]{2,1,0:T(8,128)S(1)} %all_gather.15.top_ref, bf16[320,384]{1,0:T(8,128)(2,1)S(1)} %get-tuple-element.22.rows_ref, bf16[4,768,128]{2,1,0:T(8,128)(2,1)S(1)} %fusion.3.both_ref), custom_call_target="tpu_custom_call" | custom-call | tf_op jit(solution)/shard_map/last/pallas_call | solution.py:285
  (5 shorter events, 0.1 us)
Async XLA Ops:
  0.6 27.5 %copy-start = (f32[8,128,128]{2,1,0:T(8,128)S(1)}, f32[8,128,128]{2,1,0:T(8,128)}, u32[]{:S(2)}) copy-start(f32[8,128,128]{2,1,0:T(8,128)} %param.16) | copy-start | bytes 1572868
  11.3 14.1 %copy-start.1 = (f32[4,128,128]{2,1,0:T(8,128)S(1)}, f32[4,128,128]{2,1,0:T(8,128)}, u32[]{:S(2)}) copy-start(f32[4,128,128]{2,1,0:T(8,128)} %param.14) | copy-start | bytes 786436
  11.3 20.5 %all-to-all-start = ((f32[64,8,128]{2,1,0:T(8,128)}), f32[64,8,128]{2,1,0:T(8,128)S(1)}, u32[]{:S(2)}, u32[]{:S(2)}) async-start(f32[64,8,128]{2,1,0:T(8,128)} %bitcast.3), calls=%async_computation | async-start | bytes 524288 | tf_op jit(solution)/shard_map/all_to_all | solution.py:25
  26.1 1.0 %copy-start.2 = (f32[4,128,128]{2,1,0:T(8,128)S(1)}, f32[4,128,128]{2,1,0:T(8,128)}, u32[]{:S(2)}) copy-start(f32[4,128,128]{2,1,0:T(8,128)} %param.15) | copy-start | bytes 786436
  28.4 0.7 copy-start.4
  28.4 0.7 copy-start.3

commit v6 on v5

--- a/solution.py
+++ b/solution.py
@@ -7,7 +7,6 @@
 from jax.experimental.pallas import tpu as pltpu
 from jax.sharding import Mesh, PartitionSpec as P
 
-HI = lax.Precision.HIGHEST
 CAP = 4
 LANES = 128
 NT = (((1,), (1,)), ((), ()))
@@ -34,17 +33,54 @@
     return lax.dot_general(a, b, dims, preferred_element_type=F32)
 
 
+def lanes3(m):
+    high, low = split2(m)
+    return jnp.concatenate([high, high, low], axis=1)
+
+
+def left3(m):
+    high, low = split2(m)
+    return jnp.concatenate([high, low, high], axis=1)
+
+
+def rows3(m):
+    high, low = split2(m)
+    return jnp.concatenate([high, high, low], axis=0)
+
+
 def join_kernel(
-    map_hbm, target_hbm, data_hbm, coef_hbm, out_ref, map_ref, target_ref, sems, *, local, cores
+    map_hbm,
+    over_hbm,
+    target_hbm,
+    data_hbm,
+    coef_hbm,
+    inv_hbm,
+    off_hbm,
+    out_ref,
+    parent_ref,
+    forward_ref,
+    back_ref,
+    map_ref,
+    over_ref,
+    target_ref,
+    inv_ref,
+    off_ref,
+    sems,
+    *,
+    cores,
 ):
     dates, rows = data_hbm.shape
     shard = coef_hbm.shape[0]
     total = map_hbm.shape[1]
+    local = inv_hbm.shape[0]
     copies = [
         pltpu.make_async_copy(map_hbm, map_ref, sems.at[0]),
         pltpu.make_async_copy(target_hbm, target_ref, sems.at[1]),
-        pltpu.make_async_copy(data_hbm, out_ref.at[pl.ds(0, dates)], sems.at[2]),
-        pltpu.make_async_copy(coef_hbm, out_ref.at[pl.ds(dates, shard)], sems.at[3]),
+        pltpu.make_async_copy(inv_hbm, inv_ref, sems.at[2]),
+        pltpu.make_async_copy(off_hbm, off_ref, sems.at[3]),
+        pltpu.make_async_copy(data_hbm, out_ref.at[pl.ds(0, dates)], sems.at[4]),
+        pltpu.make_async_copy(coef_hbm, out_ref.at[pl.ds(dates, shard)], sems.at[5]),
+        pltpu.make_async_copy(over_hbm, over_ref, sems.at[6]),
     ]
     for copy in copies:
         copy.start()
@@ -74,6 +110,19 @@
     )
     copies[2].wait()
     copies[3].wait()
+    for k in range(local):
+        inv = inv_ref[k]
+        product = dot(left3(off_ref[k]), rows3(inv), NN)
+        forward_ref[k] = jnp.concatenate([lanes3(product), lanes3(inv)], axis=0)
+        back_ref[k] = jnp.concatenate([rows3(inv), rows3(-product)], axis=0)
+    copies[6].wait()
+    held = parent_ref.shape[0]
+    places = lax.axis_index("chip") * held + lax.broadcasted_iota(I32, (held, total), 0)
+    over = jnp.where(where_to == places, over_ref[...], 0).astype(F32)
+    parent = jnp.sum(over, axis=1, keepdims=True).astype(I32)
+    parent_ref[...] = jnp.broadcast_to(parent, parent_ref.shape)
+    copies[4].wait()
+    copies[5].wait()
 
 
 def pack_kernel(pair_ref, out_ref, *, code_row):
@@ -97,24 +146,22 @@
         share_ref[i] = turned[dates : dates + shard, :]
 
 
-def forward_kernel(turned_ref, coef_ref, comb_ref, rows_ref, update_ref, *, shard):
+def forward_kernel(turned_ref, coef_ref, by_ref, rows_ref, update_ref, *, shard):
     local, dates, _ = update_ref.shape
     data = turned_ref[0:dates, :]
     mark = turned_ref[dates + shard : dates + shard + 1, :]
     planes = coef_ref.shape[0]
     order = [coef_ref[i ^ (planes // 2)] for i in range(planes)]
-    coef_high, coef_low = split2(jnp.concatenate(order, axis=0))
-    coef = jnp.concatenate([coef_high, coef_high, coef_low], axis=1)
     picked = jnp.concatenate(
         [jnp.where(mark == float(k + 1), data, 0.0) for k in range(local)], axis=0
     )
-    high, low = split2(picked)
-    rhs = dot(jnp.concatenate([high, low, high], axis=1), coef, NT)
-    high, low = split2(rhs)
-    rows = jnp.concatenate([high, low, high], axis=1)
-    rows_ref[...] = rows
+    rhs = left3(dot(left3(picked), lanes3(jnp.concatenate(order, axis=0)), NT))
+    width = update_ref.shape[2]
     for k in range(local):
-        update_ref[k] = dot(rows[k * dates : (k + 1) * dates], comb_ref[k], NN)
+        part = slice(k * dates, (k + 1) * dates)
+        both = dot(rhs[part], by_ref[k], NT)
+        update_ref[k] = both[:, :width]
+        rows_ref[part, :] = left3(both[:, width:])
 
 
 def reduce_kernel(both_ref, parent_ref, out_ref):
@@ -128,37 +175,41 @@
         out_ref[p] = acc
 
 
-def middle_kernel(got_ref, rhs_ref, gram_ref, out_ref):
-    pieces, width = rhs_ref.shape
+def middle_kernel(got_ref, rhs_ref, inv_ref, out_ref, *, pieces):
     chips = got_ref.shape[0] // pieces
+    tops, dates, width = rhs_ref.shape
+    half = tops * pieces * chips // (tops * dates)
+    span = dates // pieces
+    piece = lax.axis_index("chip") ^ far_index(chips)
+    p = lax.axis_index("core") * half + piece // span
     sums = [
         jnp.sum(got_ref[pl.ds(k, chips, stride=pieces), :], axis=0, keepdims=True)
         for k in range(pieces)
     ]
-    left = rhs_ref[...] - jnp.concatenate(sums, axis=0)
+    left = rhs_ref[p, pl.ds((piece % span) * pieces, pieces), :] - jnp.concatenate(sums, axis=0)
     left = jnp.concatenate([left, jnp.zeros((8 - pieces % 8, width), F32)], axis=0)
-    high, low = split2(left)
-    sol = dot(jnp.concatenate([high, low, high], axis=1), gram_ref[...], NN)
+    inv = inv_ref[p]
+    sol = dot(left3(dot(left3(left), lanes3(inv), NT)), rows3(inv), NN)
     for k in range(pieces):
         out_ref[pl.ds(k, chips, stride=pieces), :] = jnp.broadcast_to(
             sol[k : k + 1, :], (chips, width)
         )
 
 
-def last_kernel(parent_ref, top_ref, rows_ref, both_ref, out_hbm, top_hbm, out_ref, sems):
+def last_kernel(parent_ref, top_ref, rows_ref, by_ref, out_hbm, top_hbm, out_ref, sems):
     local, dates, _ = out_ref.shape
     tops = top_ref.shape[0]
     copy_top = pltpu.make_async_copy(top_ref, top_hbm, sems.at[0])
     copy_top.start()
+    first = lax.axis_index("core") * local
     copies = []
     for k in range(local):
-        parent = parent_ref[k : k + 1, :]
+        parent = parent_ref[pl.ds(first + k, 1), :]
         x = jnp.where(parent == 0, top_ref[0], 0.0)
         for p in range(1, tops):
             x = jnp.where(parent == p, top_ref[p], x)
-        high, low = split2(x)
         rows = rows_ref[k * dates : (k + 1) * dates, :]
-        out_ref[k] = dot(jnp.concatenate([rows, high, low, high], axis=1), both_ref[k], NN)
+        out_ref[k] = dot(jnp.concatenate([rows, left3(x)], axis=1), by_ref[k], NN)
         copies.append(pltpu.make_async_copy(out_ref.at[k], out_hbm.at[k], sems.at[1 + k]))
         copies[-1].start()
     copy_top.wait()
@@ -176,13 +227,6 @@
 
 def vmem(*arrays):
     return [pltpu.with_memory_space_constraint(a, pltpu.VMEM) for a in arrays]
-
-
-def triple(m):
-    high = lax.reduce_precision(m, 8, 7)
-    low = (m - high).astype(BF16)
-    high = high.astype(BF16)
-    return jnp.concatenate([high, high, low], axis=-2)
 
 
 def body(
@@ -191,8 +235,6 @@
     chips = lax.axis_size("chip")
     cores = lax.axis_size("core")
     planes = lax.axis_size("rhs")
-    q = lax.axis_index("chip")
-    c = lax.axis_index("core")
     local = leaf_inv.shape[0]
     width = leaf_inv.shape[1]
     tops = top_inv.shape[0]
@@ -203,22 +245,37 @@
     n_slots = chips * slots
     half = tops // cores
     pieces = half * dates // chips
-    span = dates // pieces
     height = dates + shard + 8
     far = far_index(chips)
 
-    payload = pl.pallas_call(
-        lambda *refs: join_kernel(*refs, local=local, cores=cores),
-        out_shape=arr(height, rows),
-        in_specs=[ANY, ANY, ANY, ANY],
-        out_specs=VM,
+    payload, parent, forward_by, back_by = pl.pallas_call(
+        lambda *refs: join_kernel(*refs, cores=cores),
+        out_shape=(
+            arr(height, rows),
+            pltpu.VMEM((cores * local, LANES), I32),
+            pltpu.VMEM((local, 2 * width, 3 * width), BF16),
+            pltpu.VMEM((local, 6 * width, width), BF16),
+        ),
+        in_specs=[ANY] * 7,
+        out_specs=(VM, VM, VM, VM),
         scratch_shapes=[
             pltpu.VMEM((1, total), I32),
+            pltpu.VMEM((1, total), I32),
             pltpu.VMEM((1, rows), I32),
-            pltpu.SemaphoreType.DMA((4,)),
+            pltpu.VMEM((local, width, width), F32),
+            pltpu.VMEM((local, width, width), F32),
+            pltpu.SemaphoreType.DMA((7,)),
         ],
         name="join",
-    )(leaf_map.reshape(1, total), obs_target.reshape(1, rows), obs_data, obs_coef)
+    )(
+        leaf_map.reshape(1, total),
+        leaf_parent.reshape(1, total),
+        obs_target.reshape(1, rows),
+        obs_data,
+        obs_coef,
+        leaf_inv,
+        leaf_off,
+    )
     pair = lax.all_gather(payload, "core", axis=0)
     placed = pl.pallas_call(
         lambda *refs: pack_kernel(*refs, code_row=dates + shard + 1),
@@ -228,26 +285,6 @@
         name="pack",
     )(*vmem(pair))
     recv = exchange(placed.reshape(chips, slots, LANES), "chip", far)
-
-    update_by = triple(jnp.einsum("lcd,lde->lec", leaf_off, leaf_inv, precision=HI))
-    product = jnp.einsum("lcd,lde->lce", leaf_off, leaf_inv, precision=HI)
-    square = jnp.einsum("ldc,lde->lce", leaf_inv, leaf_inv, precision=HI)
-    solve_by = jnp.concatenate([triple(square), triple(-product)], axis=1)
-    places = q * (cores * local) + jnp.arange(cores * local, dtype=I32)
-    held = leaf_map[None, :] == places[:, None]
-    parent = jnp.sum(jnp.where(held, leaf_parent[None, :], 0), axis=1)
-    own_parent = lax.dynamic_slice_in_dim(parent, c * local, local, 0)
-    parent = jnp.broadcast_to(parent[:, None], (cores * local, LANES))
-    own_parent = jnp.broadcast_to(own_parent[:, None], (local, LANES))
-    piece = q ^ far
-    p = c * half + piece // span
-    own_inv = lax.dynamic_index_in_dim(top_inv, p, 0, keepdims=False)
-    gram = triple(lax.dot_general(own_inv, own_inv, (((0,), (0,)), ((), ())), precision=HI))
-    own_rhs = lax.dynamic_slice(top_rhs, (p, (piece % span) * pieces, 0), (1, pieces, width))
-    own_rhs = own_rhs.reshape(pieces, width)
-    recv, update_by, solve_by, parent, own_parent, gram, own_rhs = lax.optimization_barrier(
-        (recv, update_by, solve_by, parent, own_parent, gram, own_rhs)
-    )
 
     turned, share = pl.pallas_call(
         lambda *refs: turn_kernel(*refs, dates=dates),
@@ -263,7 +300,7 @@
         in_specs=[VM, VM, VM],
         out_specs=(VM, VM),
         name="forward",
-    )(*vmem(turned, coef, update_by))
+    )(*vmem(turned, coef, forward_by))
     both = lax.all_gather(update, "core", axis=0, tiled=True)
     contrib = pl.pallas_call(
         reduce_kernel,
@@ -274,12 +311,12 @@
     )(*vmem(both, parent))
     got = exchange(contrib.reshape(chips, 1, pieces * width), "chip", far)
     out = pl.pallas_call(
-        middle_kernel,
+        lambda *refs: middle_kernel(*refs, pieces=pieces),
         out_shape=arr(chips * pieces, width),
         in_specs=[VM, VM, VM],
         out_specs=VM,
         name="middle",
-    )(*vmem(got.reshape(chips * pieces, width), own_rhs, gram))
+    )(*vmem(got.reshape(chips * pieces, width), top_rhs, top_inv))
     full = exchange(out.reshape(chips, 1, pieces * width), "chip", far)
     full = lax.all_gather(full.reshape(half, dates, width), "core", axis=0, tiled=True)
     return pl.pallas_call(
@@ -295,7 +332,7 @@
             pltpu.SemaphoreType.DMA((1 + local,)),
         ],
         name="last",
-    )(*vmem(own_parent, full, parts, solve_by))
+    )(*vmem(parent, full, parts, back_by))
 
 
 def solution(mesh):

time: 82 us -> 81.9 us (level)
  blocking collectives: 56 us -> 76.5 us
  starting transfers between devices: 14.1 us -> 0 us
  local copies, waits for them, and re-layouts: 2.51 us -> 0.01 us
  matrix products: 1.91 us -> 0 us
  waiting for transfers between devices: 1.56 us -> 0 us
    all_to_all x3 -> x4, blocking collectives: 39.8 us -> 60 us  [exchange(): return lax.all_to_all(x, axis, 0, 0, axis_index_groups=[order])]
    all_to_all x1 -> x0, starting transfers between devices: 14.1 us -> none  [exchange(): return lax.all_to_all(x, axis, 0, 0, axis_index_groups=[order])]
    dot_general x4 -> x0, matrix products: 1.91 us -> none  [the longest x1 0.6 us: body(): jnp.einsum('lcd,lde->lec', leaf_off, leaf_inv, precision=HI)]
    unnamed x10 -> x4, local copies, waits for them, and re-layouts: 1.58 us -> 0.01 us
    all_to_all x1 -> x0, waiting for transfers between devices: 1.56 us -> none  [exchange(): return lax.all_to_all(x, axis, 0, 0, axis_index_groups=[order])]
  transfers between devices with their start and end apart: 1 -> 0, of which waited for: 1 -> 0; matrix products, arithmetic and copies ran while one was open for 4% -> 0% of each run, Pallas kernels for 0% -> 0%
where the time goes in v6:
time: 81.9 us; the launch traced here: 81.6 us
  blocking collectives  76.5 us (93%)
  Pallas kernels  4.45 us (5%)
    all_to_all x4, blocking collectives, exchange(): return lax.all_to_all(x, axis, 0, 0, axis_index_groups=[order])  60 us
    all_gather x1, blocking collectives, body(): pair = lax.all_gather(payload, 'core', axis=0)  8.46 us
    all_gather x1, blocking collectives, body(): lax.all_gather(full.reshape(half, dates, width), 'core', axis=0, tiled=True)  4.26 us
    all_gather x1, blocking collectives, body(): both = lax.all_gather(update, 'core', axis=0, tiled=True)  3.69 us

profile of v6, /device:TPU:1, one launch (start us, length us, event | category | flops | bytes accessed | tf_op | source)
XLA Modules:
  0.0 81.6 jit_solution(337760744850801880)
XLA Ops:
  0.6 1.5 %join.1 = (f32[120,256]{1,0:T(8,128)S(1)}, s32[8,128]{1,0:T(8,128)S(1)}, bf16[4,256,384]{2,1,0:T(8,128)(2,1)S(1)}, bf16[4,768,128]{2,1,0:T(8,128)(2,1)S(1)}) custom-call(s32[1,512]{1,0:T(1,128)} %bitcast.17, s32[1,512]{1,0:T(1,128)} %bitcast.18, s32[1,256]{1,0:T(1,128)} %bitcast.19, f32[80,256]{1,0:T(8,128)} %refs_3_.1, f32[32,256]{1,0:T(8,128)} %refs_4_.1, ...), custom_call_target="tpu_custom_call" | custom-call | tf_op jit(solution)/shard_map/join/pallas_call | solution.py:251
  2.1 8.5 %all-gather = f32[240,256]{1,0:T(8,128)S(1)} all-gather(f32[120,256]{1,0:T(8,128)S(1)} %get-tuple-element.11), channel_id=2, replica_groups=mesh['chip'=64,'core'=2,'rhs'=4] {'core'}, dimensions={0}, use_global_device_ids=true | all-gather | bytes 368640 | tf_op jit(solution)/shard_map/all_gather | solution.py:279
  10.6 0.3 pack.1
  10.9 20.1 %all_to_all.20 = f32[64,8,128]{2,1,0:T(8,128)S(1)} all-to-all(f32[64,8,128]{2,1,0:T(8,128)S(1)} %bitcast.11), channel_id=1, replica_groups={{288,296,304,312,256,264,272,280,352,360,368,376,320,328,336,344,416,42..., dimensions={0} | all-to-all | bytes 524288 | tf_op jit(solution)/shard_map/all_to_all | solution.py:24
  31.1 0.1 turn.1
  31.2 8.3 %all_to_all.21.refs_1_ = f32[4,32,512]{2,1,0:T(8,128)S(1)} all-to-all(f32[4,32,512]{2,1,0:T(8,128)S(1)} %get-tuple-element.13), channel_id=1, replica_groups={{2,3,0,1},{6,7,4,5},{10,11,8,9},{14,15,12,13},{18,19,16,17},{22,23,20,2..., dimensions={0} | all-to-all | bytes 524288 | tf_op jit(solution)/shard_map/all_to_all | solution.py:24
  39.5 1.1 %forward.1 = (bf16[320,384]{1,0:T(8,128)(2,1)S(1)}, f32[4,80,128]{2,1,0:T(8,128)S(1)}) custom-call(f32[128,512]{1,0:T(8,128)S(1)} %get-tuple-element.12.refs_0_, f32[4,32,512]{2,1,0:T(8,128)S(1)} %all_to_all.21.refs_1_, bf16[4,256,384]{2,1,0:T(8,128)(2,1)S(1)} %get-tuple-element.14.refs_2_), custom_call_target="tpu_custom_call" | custom-call | tf_op jit(solution)/shard_map/forward/pallas_call | solution.py:297
  40.5 0.0 copy-start.1
  40.6 3.7 %all_gather.14.both_ref = f32[8,80,128]{2,1,0:T(8,128)S(1)} all-gather(f32[4,80,128]{2,1,0:T(8,128)S(1)} %get-tuple-element.15), channel_id=1, replica_groups=mesh['chip'=64,'core'=2,'rhs'=4] {'core'}, dimensions={0}, use_global_device_ids=true | all-gather | bytes 491520 | tf_op jit(solution)/shard_map/all_gather | solution.py:304
  44.3 0.0 copy-start
  44.3 0.1 reduce.1
  44.4 16.4 %all_to_all.22 = f32[64,1,640]{2,1,0:T(1,128)S(1)} all-to-all(f32[64,1,640]{2,1,0:T(1,128)S(1)} %bitcast.15), channel_id=1, replica_groups={{288,296,304,312,256,264,272,280,352,360,368,376,320,328,336,344,416,42..., dimensions={0} | all-to-all | bytes 327680 | tf_op jit(solution)/shard_map/all_to_all | solution.py:24
  60.7 0.0 copy-done.1
  60.7 0.0 copy-done
  60.7 0.3 middle.1
  61.1 15.3 %all_to_all.23 = f32[64,1,640]{2,1,0:T(1,128)S(1)} all-to-all(f32[64,1,640]{2,1,0:T(1,128)S(1)} %bitcast.14), channel_id=1, replica_groups={{288,296,304,312,256,264,272,280,352,360,368,376,320,328,336,344,416,42..., dimensions={0} | all-to-all | bytes 327680 | tf_op jit(solution)/shard_map/all_to_all | solution.py:24
  76.4 4.3 %all_gather.15.top_ref = f32[8,80,128]{2,1,0:T(8,128)S(1)} all-gather(f32[4,80,128]{2,1,0:T(8,128)S(1)} %bitcast.16), channel_id=1, replica_groups=mesh['chip'=64,'core'=2,'rhs'=4] {'core'}, dimensions={0}, use_global_device_ids=true | all-gather | bytes 491520 | tf_op jit(solution)/shard_map/all_gather | solution.py:321
  80.6 1.0 %last.1 = (f32[4,80,128]{2,1,0:T(8,128)}, f32[8,80,128]{2,1,0:T(8,128)}) custom-call(s32[8,128]{1,0:T(8,128)S(1)} %get-tuple-element.10.parent_ref, f32[8,80,128]{2,1,0:T(8,128)S(1)} %all_gather.15.top_ref, bf16[320,384]{1,0:T(8,128)(2,1)S(1)} %get-tuple-element.16.rows_ref, bf16[4,768,128]{2,1,0:T(8,128)(2,1)S(1)} %get-tuple-element.17.by_ref), custom_call_target="tpu_custom_call" | custom-call | tf_op jit(solution)/shard_map/last/pallas_call | solution.py:322
Async XLA Ops:
  40.5 20.2 %copy-start.1 = (f32[8,80,128]{2,1,0:T(8,128)S(1)}, f32[8,80,128]{2,1,0:T(8,128)}, u32[]{:S(2)}) copy-start(f32[8,80,128]{2,1,0:T(8,128)} %refs_1_.1) | copy-start | bytes 983044
  44.3 16.5 %copy-start = (f32[8,128,128]{2,1,0:T(8,128)S(1)}, f32[8,128,128]{2,1,0:T(8,128)}, u32[]{:S(2)}) copy-start(f32[8,128,128]{2,1,0:T(8,128)} %refs_2_.1) | copy-start | bytes 1572868

commit v7 on v6

--- a/solution.py
+++ b/solution.py
@@ -46,6 +46,20 @@
 def rows3(m):
     high, low = split2(m)
     return jnp.concatenate([high, high, low], axis=0)
+
+
+def late_start(chips):
+    side = math.isqrt(chips)
+    q = lax.axis_index("chip")
+    return jnp.abs(q // side - side // 2) + jnp.abs(q % side - side // 2) <= side // 2
+
+
+def fill_back(inv_ref, off_ref, back_ref):
+    for k in range(inv_ref.shape[0]):
+        inv = inv_ref[k]
+        square = dot(left3(inv.T), rows3(inv), NN)
+        product = dot(left3(off_ref[k]), rows3(inv), NN)
+        back_ref[k] = jnp.concatenate([rows3(square), rows3(-product)], axis=0)
 
 
 def join_kernel(
@@ -111,10 +125,7 @@
     copies[2].wait()
     copies[3].wait()
     for k in range(local):
-        inv = inv_ref[k]
-        product = dot(left3(off_ref[k]), rows3(inv), NN)
-        forward_ref[k] = jnp.concatenate([lanes3(product), lanes3(inv)], axis=0)
-        back_ref[k] = jnp.concatenate([rows3(inv), rows3(-product)], axis=0)
+        forward_ref[k] = lanes3(dot(left3(off_ref[k]), rows3(inv_ref[k]), NN))
     copies[6].wait()
     held = parent_ref.shape[0]
     places = lax.axis_index("chip") * held + lax.broadcasted_iota(I32, (held, total), 0)
@@ -123,6 +134,10 @@
     parent_ref[...] = jnp.broadcast_to(parent, parent_ref.shape)
     copies[4].wait()
     copies[5].wait()
+
+    @pl.when(jnp.logical_not(late_start(chips)))
+    def _():
+        fill_back(inv_ref, off_ref, back_ref)
 
 
 def pack_kernel(pair_ref, out_ref, *, code_row):
@@ -156,12 +171,9 @@
         [jnp.where(mark == float(k + 1), data, 0.0) for k in range(local)], axis=0
     )
     rhs = left3(dot(left3(picked), lanes3(jnp.concatenate(order, axis=0)), NT))
-    width = update_ref.shape[2]
+    rows_ref[...] = rhs
     for k in range(local):
-        part = slice(k * dates, (k + 1) * dates)
-        both = dot(rhs[part], by_ref[k], NT)
-        update_ref[k] = both[:, :width]
-        rows_ref[part, :] = left3(both[:, width:])
+        update_ref[k] = dot(rhs[k * dates : (k + 1) * dates], by_ref[k], NT)
 
 
 def reduce_kernel(both_ref, parent_ref, out_ref):
@@ -196,25 +208,51 @@
         )
 
 
-def last_kernel(parent_ref, top_ref, rows_ref, by_ref, out_hbm, top_hbm, out_ref, sems):
+def last_kernel(
+    parent_ref,
+    top_ref,
+    rows_ref,
+    back_ref,
+    inv_ref,
+    off_ref,
+    out_hbm,
+    top_hbm,
+    out_ref,
+    own_ref,
+    sems,
+    *,
+    chips,
+):
     local, dates, _ = out_ref.shape
     tops = top_ref.shape[0]
     copy_top = pltpu.make_async_copy(top_ref, top_hbm, sems.at[0])
     copy_top.start()
     first = lax.axis_index("core") * local
-    copies = []
+
+    def solve(by_ref):
+        for k in range(local):
+            parent = parent_ref[pl.ds(first + k, 1), :]
+            x = jnp.where(parent == 0, top_ref[0], 0.0)
+            for p in range(1, tops):
+                x = jnp.where(parent == p, top_ref[p], x)
+            rows = rows_ref[k * dates : (k + 1) * dates, :]
+            out_ref[k] = dot(jnp.concatenate([rows, left3(x)], axis=1), by_ref[k], NN)
+            pltpu.make_async_copy(out_ref.at[k], out_hbm.at[k], sems.at[1 + k]).start()
+
+    late = late_start(chips)
+
+    @pl.when(late)
+    def _():
+        fill_back(inv_ref, off_ref, own_ref)
+        solve(own_ref)
+
+    @pl.when(jnp.logical_not(late))
+    def _():
+        solve(back_ref)
+
+    copy_top.wait()
     for k in range(local):
-        parent = parent_ref[pl.ds(first + k, 1), :]
-        x = jnp.where(parent == 0, top_ref[0], 0.0)
-        for p in range(1, tops):
-            x = jnp.where(parent == p, top_ref[p], x)
-        rows = rows_ref[k * dates : (k + 1) * dates, :]
-        out_ref[k] = dot(jnp.concatenate([rows, left3(x)], axis=1), by_ref[k], NN)
-        copies.append(pltpu.make_async_copy(out_ref.at[k], out_hbm.at[k], sems.at[1 + k]))
-        copies[-1].start()
-    copy_top.wait()
-    for copy in copies:
-        copy.wait()
+        pltpu.make_async_copy(out_ref.at[k], out_hbm.at[k], sems.at[1 + k]).wait()
 
 
 VM = pl.BlockSpec(memory_space=pltpu.VMEM)
@@ -253,11 +291,11 @@
         out_shape=(
             arr(height, rows),
             pltpu.VMEM((cores * local, LANES), I32),
-            pltpu.VMEM((local, 2 * width, 3 * width), BF16),
+            pltpu.VMEM((local, width, 3 * width), BF16),
             pltpu.VMEM((local, 6 * width, width), BF16),
         ),
         in_specs=[ANY] * 7,
-        out_specs=(VM, VM, VM, VM),
+        out_specs=(VM,) * 4,
         scratch_shapes=[
             pltpu.VMEM((1, total), I32),
             pltpu.VMEM((1, total), I32),
@@ -320,19 +358,20 @@
     full = exchange(out.reshape(chips, 1, pieces * width), "chip", far)
     full = lax.all_gather(full.reshape(half, dates, width), "core", axis=0, tiled=True)
     return pl.pallas_call(
-        last_kernel,
+        lambda *refs: last_kernel(*refs, chips=chips),
         out_shape=(
             jax.ShapeDtypeStruct((local, dates, width), F32),
             jax.ShapeDtypeStruct((tops, dates, width), F32),
         ),
-        in_specs=[VM, VM, VM, VM],
+        in_specs=[VM] * 6,
         out_specs=(ANY, ANY),
         scratch_shapes=[
             pltpu.VMEM((local, dates, width), F32),
+            pltpu.VMEM((local, 6 * width, width), BF16),
             pltpu.SemaphoreType.DMA((1 + local,)),
         ],
         name="last",
-    )(*vmem(parent, full, parts, back_by))
+    )(*vmem(parent, full, parts, back_by, leaf_inv, leaf_off))
 
 
 def solution(mesh):

time: 81.9 us -> 82.4 us (level)
  no operation moved by 1% of the time
where the time goes in v7:
time: 82.4 us; the launch traced here: 82.1 us
  blocking collectives  76.7 us (93%)
  Pallas kernels  4.63 us (6%)
    all_to_all x4, blocking collectives, exchange(): return lax.all_to_all(x, axis, 0, 0, axis_index_groups=[order])  60.2 us
    all_gather x1, blocking collectives, body(): pair = lax.all_gather(payload, 'core', axis=0)  8.46 us
    all_gather x1, blocking collectives, body(): lax.all_gather(full.reshape(half, dates, width), 'core', axis=0, tiled=True)  4.39 us
    all_gather x1, blocking collectives, body(): both = lax.all_gather(update, 'core', axis=0, tiled=True)  3.7 us
    pallas_call x1, Pallas kernels, body(): pl.pallas_call(lambda *refs: join_kernel(*refs, cores=cores), out_shape=(...  1.92 us

profile of v7, /device:TPU:1, one launch (start us, length us, event | category | flops | bytes accessed | tf_op | source)
XLA Modules:
  0.0 82.1 jit_solution(9976649081545009671)
XLA Ops:
  0.6 1.9 %join.1 = (f32[120,256]{1,0:T(8,128)S(1)}, s32[8,128]{1,0:T(8,128)S(1)}, bf16[4,128,384]{2,1,0:T(8,128)(2,1)S(1)}, bf16[4,768,128]{2,1,0:T(8,128)(2,1)S(1)}) custom-call(s32[1,512]{1,0:T(1,128)} %bitcast.17, s32[1,512]{1,0:T(1,128)} %bitcast.18, s32[1,256]{1,0:T(1,128)} %bitcast.19, f32[80,256]{1,0:T(8,128)} %refs_3_.1, f32[32,256]{1,0:T(8,128)} %refs_4_.2, ...), custom_call_target="tpu_custom_call" | custom-call | tf_op jit(solution)/shard_map/join/pallas_call | solution.py:289
  2.6 8.5 %all-gather = f32[240,256]{1,0:T(8,128)S(1)} all-gather(f32[120,256]{1,0:T(8,128)S(1)} %get-tuple-element.11), channel_id=2, replica_groups=mesh['chip'=64,'core'=2,'rhs'=4] {'core'}, dimensions={0}, use_global_device_ids=true | all-gather | bytes 368640 | tf_op jit(solution)/shard_map/all_gather | solution.py:317
  11.0 0.3 pack.1
  11.3 20.1 %all_to_all.20 = f32[64,8,128]{2,1,0:T(8,128)S(1)} all-to-all(f32[64,8,128]{2,1,0:T(8,128)S(1)} %bitcast.11), channel_id=1, replica_groups={{288,296,304,312,256,264,272,280,352,360,368,376,320,328,336,344,416,42..., dimensions={0} | all-to-all | bytes 524288 | tf_op jit(solution)/shard_map/all_to_all | solution.py:24
  31.5 0.1 turn.1
  31.6 8.3 %all_to_all.21.refs_1_ = f32[4,32,512]{2,1,0:T(8,128)S(1)} all-to-all(f32[4,32,512]{2,1,0:T(8,128)S(1)} %get-tuple-element.13), channel_id=1, replica_groups={{2,3,0,1},{6,7,4,5},{10,11,8,9},{14,15,12,13},{18,19,16,17},{22,23,20,2..., dimensions={0} | all-to-all | bytes 524288 | tf_op jit(solution)/shard_map/all_to_all | solution.py:24
  39.9 0.8 %forward.1 = (bf16[320,384]{1,0:T(8,128)(2,1)S(1)}, f32[4,80,128]{2,1,0:T(8,128)S(1)}) custom-call(f32[128,512]{1,0:T(8,128)S(1)} %get-tuple-element.12.refs_0_, f32[4,32,512]{2,1,0:T(8,128)S(1)} %all_to_all.21.refs_1_, bf16[4,128,384]{2,1,0:T(8,128)(2,1)S(1)} %get-tuple-element.14.refs_2_), custom_call_target="tpu_custom_call" | custom-call | tf_op jit(solution)/shard_map/forward/pallas_call | solution.py:335
  40.7 0.0 copy-start.3
  40.7 3.7 %all_gather.14.both_ref = f32[8,80,128]{2,1,0:T(8,128)S(1)} all-gather(f32[4,80,128]{2,1,0:T(8,128)S(1)} %get-tuple-element.15), channel_id=1, replica_groups=mesh['chip'=64,'core'=2,'rhs'=4] {'core'}, dimensions={0}, use_global_device_ids=true | all-gather | bytes 491520 | tf_op jit(solution)/shard_map/all_gather | solution.py:342
  44.4 0.0 copy-start.2
  44.4 0.1 reduce.1
  44.6 16.4 %all_to_all.22 = f32[64,1,640]{2,1,0:T(1,128)S(1)} all-to-all(f32[64,1,640]{2,1,0:T(1,128)S(1)} %bitcast.15), channel_id=1, replica_groups={{288,296,304,312,256,264,272,280,352,360,368,376,320,328,336,344,416,42..., dimensions={0} | all-to-all | bytes 327680 | tf_op jit(solution)/shard_map/all_to_all | solution.py:24
  60.9 0.0 copy-done.3
  60.9 0.0 copy-done.2
  60.9 0.3 middle.1
  61.3 0.0 copy-start.1
  61.3 15.4 %all_to_all.23 = f32[64,1,640]{2,1,0:T(1,128)S(1)} all-to-all(f32[64,1,640]{2,1,0:T(1,128)S(1)} %bitcast.14), channel_id=1, replica_groups={{288,296,304,312,256,264,272,280,352,360,368,376,320,328,336,344,416,42..., dimensions={0} | all-to-all | bytes 327680 | tf_op jit(solution)/shard_map/all_to_all | solution.py:24
  76.7 0.0 copy-start
  76.7 4.4 %all_gather.15.refs_1_ = f32[8,80,128]{2,1,0:T(8,128)S(1)} all-gather(f32[4,80,128]{2,1,0:T(8,128)S(1)} %bitcast.16), channel_id=1, replica_groups=mesh['chip'=64,'core'=2,'rhs'=4] {'core'}, dimensions={0}, use_global_device_ids=true | all-gather | bytes 491520 | tf_op jit(solution)/shard_map/all_gather | solution.py:359
  81.1 0.0 copy-done.1
  81.1 0.0 copy-done
  81.1 1.0 %last.1 = (f32[4,80,128]{2,1,0:T(8,128)}, f32[8,80,128]{2,1,0:T(8,128)}) custom-call(s32[8,128]{1,0:T(8,128)S(1)} %get-tuple-element.10.parent_ref.refs_0_, f32[8,80,128]{2,1,0:T(8,128)S(1)} %all_gather.15.refs_1_, bf16[320,384]{1,0:T(8,128)(2,1)S(1)} %get-tuple-element.16.refs_2_, bf16[4,768,128]{2,1,0:T(8,128)(2,1)S(1)} %get-tuple-element.17.refs_3_, ...), custom_call_target="tpu_custom_call" | custom-call | tf_op jit(solution)/shard_map/last/pallas_call | solution.py:360
Async XLA Ops:
  40.7 20.2 %copy-start.3 = (f32[8,80,128]{2,1,0:T(8,128)S(1)}, f32[8,80,128]{2,1,0:T(8,128)}, u32[]{:S(2)}) copy-start(f32[8,80,128]{2,1,0:T(8,128)} %refs_1_.1) | copy-start | bytes 983044
  44.4 16.5 %copy-start.2 = (f32[8,128,128]{2,1,0:T(8,128)S(1)}, f32[8,128,128]{2,1,0:T(8,128)}, u32[]{:S(2)}) copy-start(f32[8,128,128]{2,1,0:T(8,128)} %refs_2_.1) | copy-start | bytes 1572868
  61.3 19.8 %copy-start.1 = (f32[4,128,128]{2,1,0:T(8,128)S(1)}, f32[4,128,128]{2,1,0:T(8,128)}, u32[]{:S(2)}) copy-start(f32[4,128,128]{2,1,0:T(8,128)} %refs_5_.3) | copy-start | bytes 786436
  76.7 4.4 %copy-start = (f32[4,128,128]{2,1,0:T(8,128)S(1)}, f32[4,128,128]{2,1,0:T(8,128)}, u32[]{:S(2)}) copy-start(f32[4,128,128]{2,1,0:T(8,128)} %refs_4_.3) | copy-start | bytes 786436

commit v8 on v5

--- a/solution.py
+++ b/solution.py
@@ -35,7 +35,20 @@
 
 
 def join_kernel(
-    map_hbm, target_hbm, data_hbm, coef_hbm, out_ref, map_ref, target_ref, sems, *, local, cores
+    map_hbm,
+    target_hbm,
+    data_hbm,
+    coef_hbm,
+    over_hbm,
+    out_ref,
+    parent_ref,
+    map_ref,
+    target_ref,
+    over_ref,
+    sems,
+    *,
+    local,
+    cores,
 ):
     dates, rows = data_hbm.shape
     shard = coef_hbm.shape[0]
@@ -45,6 +58,7 @@
         pltpu.make_async_copy(target_hbm, target_ref, sems.at[1]),
         pltpu.make_async_copy(data_hbm, out_ref.at[pl.ds(0, dates)], sems.at[2]),
         pltpu.make_async_copy(coef_hbm, out_ref.at[pl.ds(dates, shard)], sems.at[3]),
+        pltpu.make_async_copy(over_hbm, over_ref, sems.at[4]),
     ]
     for copy in copies:
         copy.start()
@@ -72,21 +86,37 @@
     out_ref[dates + shard :, :] = jnp.concatenate(
         [found[1:2, :] + 1.0, code.astype(F32), jnp.zeros((tail - 2, rows), F32)], axis=0
     )
+    copies[4].wait()
+    held = parent_ref.shape[0]
+    places = lax.axis_index("chip") * held + lax.broadcasted_iota(I32, (held, total), 0)
+    over = jnp.where(where_to == places, over_ref[...], 0).astype(F32)
+    parent = jnp.sum(over, axis=1, keepdims=True).astype(I32)
+    parent_ref[...] = jnp.broadcast_to(parent, parent_ref.shape)
     copies[2].wait()
     copies[3].wait()
 
 
-def pack_kernel(pair_ref, out_ref, *, code_row):
+def pack_kernel(pair_ref, out_hbm, out_ref, sems, *, code_row):
     cores, height, rows = pair_ref.shape
     n_slots = out_ref.shape[0]
+    parts = sems.shape[0]
+    size = n_slots // parts
     code = jnp.concatenate([pair_ref[s, code_row : code_row + 1, :] for s in range(cores)], axis=1)
     code = code.astype(I32) - lax.axis_index("core") * n_slots
-    put = (lax.broadcasted_iota(I32, (n_slots, cores * rows), 0) == code).astype(F32).astype(BF16)
     rest = jnp.zeros((LANES - height, cores * rows), F32)
     feat = jnp.concatenate([pair_ref[s] for s in range(cores)], axis=1)
-    feat = jnp.concatenate([feat, rest], axis=0)
-    both = dot(put, jnp.concatenate(split2(feat), axis=0), NT)
-    out_ref[...] = both[:, :LANES] + both[:, LANES:]
+    feat = jnp.concatenate(split2(jnp.concatenate([feat, rest], axis=0)), axis=0)
+    ids = lax.broadcasted_iota(I32, (size, cores * rows), 0)
+    copies = []
+    for i in range(parts):
+        put = (ids == code - i * size).astype(F32).astype(BF16)
+        both = dot(put, feat, NT)
+        here = pl.ds(i * size, size)
+        out_ref[here, :] = both[:, :LANES] + both[:, LANES:]
+        copies.append(pltpu.make_async_copy(out_ref.at[here], out_hbm.at[here], sems.at[i]))
+        copies[-1].start()
+    for copy in copies:
+        copy.wait()
 
 
 def turn_kernel(recv_ref, turned_ref, share_ref, *, dates):
@@ -150,9 +180,10 @@
     tops = top_ref.shape[0]
     copy_top = pltpu.make_async_copy(top_ref, top_hbm, sems.at[0])
     copy_top.start()
+    first = lax.axis_index("core") * local
     copies = []
     for k in range(local):
-        parent = parent_ref[k : k + 1, :]
+        parent = parent_ref[pl.ds(first + k, 1), :]
         x = jnp.where(parent == 0, top_ref[0], 0.0)
         for p in range(1, tops):
             x = jnp.where(parent == p, top_ref[p], x)
@@ -207,24 +238,32 @@
     height = dates + shard + 8
     far = far_index(chips)
 
-    payload = pl.pallas_call(
+    payload, parent = pl.pallas_call(
         lambda *refs: join_kernel(*refs, local=local, cores=cores),
-        out_shape=arr(height, rows),
-        in_specs=[ANY, ANY, ANY, ANY],
-        out_specs=VM,
+        out_shape=(arr(height, rows), pltpu.VMEM((cores * local, LANES), I32)),
+        in_specs=[ANY] * 5,
+        out_specs=(VM, VM),
         scratch_shapes=[
             pltpu.VMEM((1, total), I32),
             pltpu.VMEM((1, rows), I32),
-            pltpu.SemaphoreType.DMA((4,)),
+            pltpu.VMEM((1, total), I32),
+            pltpu.SemaphoreType.DMA((5,)),
         ],
         name="join",
-    )(leaf_map.reshape(1, total), obs_target.reshape(1, rows), obs_data, obs_coef)
+    )(
+        leaf_map.reshape(1, total),
+        obs_target.reshape(1, rows),
+        obs_data,
+        obs_coef,
+        leaf_parent.reshape(1, total),
+    )
     pair = lax.all_gather(payload, "core", axis=0)
     placed = pl.pallas_call(
         lambda *refs: pack_kernel(*refs, code_row=dates + shard + 1),
-        out_shape=arr(n_slots, LANES),
+        out_shape=jax.ShapeDtypeStruct((n_slots, LANES), F32),
         in_specs=[VM],
-        out_specs=VM,
+        out_specs=ANY,
+        scratch_shapes=[pltpu.VMEM((n_slots, LANES), F32), pltpu.SemaphoreType.DMA((4,))],
         name="pack",
     )(*vmem(pair))
     recv = exchange(placed.reshape(chips, slots, LANES), "chip", far)
@@ -233,20 +272,14 @@
     product = jnp.einsum("lcd,lde->lce", leaf_off, leaf_inv, precision=HI)
     square = jnp.einsum("ldc,lde->lce", leaf_inv, leaf_inv, precision=HI)
     solve_by = jnp.concatenate([triple(square), triple(-product)], axis=1)
-    places = q * (cores * local) + jnp.arange(cores * local, dtype=I32)
-    held = leaf_map[None, :] == places[:, None]
-    parent = jnp.sum(jnp.where(held, leaf_parent[None, :], 0), axis=1)
-    own_parent = lax.dynamic_slice_in_dim(parent, c * local, local, 0)
-    parent = jnp.broadcast_to(parent[:, None], (cores * local, LANES))
-    own_parent = jnp.broadcast_to(own_parent[:, None], (local, LANES))
     piece = q ^ far
     p = c * half + piece // span
     own_inv = lax.dynamic_index_in_dim(top_inv, p, 0, keepdims=False)
     gram = triple(lax.dot_general(own_inv, own_inv, (((0,), (0,)), ((), ())), precision=HI))
     own_rhs = lax.dynamic_slice(top_rhs, (p, (piece % span) * pieces, 0), (1, pieces, width))
     own_rhs = own_rhs.reshape(pieces, width)
-    recv, update_by, solve_by, parent, own_parent, gram, own_rhs = lax.optimization_barrier(
-        (recv, update_by, solve_by, parent, own_parent, gram, own_rhs)
+    recv, update_by, solve_by, gram, own_rhs = lax.optimization_barrier(
+        (recv, update_by, solve_by, gram, own_rhs)
     )
 
     turned, share = pl.pallas_call(
@@ -295,7 +328,7 @@
             pltpu.SemaphoreType.DMA((1 + local,)),
         ],
         name="last",
-    )(*vmem(own_parent, full, parts, solve_by))
+    )(*vmem(parent, full, parts, solve_by))
 
 
 def solution(mesh):

time: 82 us -> 82.1 us (level)
  waiting for transfers between devices: 1.56 us -> 2.48 us
  local copies, waits for them, and re-layouts: 2.51 us -> 1.62 us
    all_to_all x1, waiting for transfers between devices: 1.56 us -> 2.48 us  [exchange(): return lax.all_to_all(x, axis, 0, 0, axis_index_groups=[order])]
where the time goes in v8:
time: 82.1 us; the launch traced here: 81.7 us
  blocking collectives  56.1 us (68%)
  starting transfers between devices  14.1 us (17%)
  Pallas kernels  4.48 us (5%)
  waiting for transfers between devices  2.48 us (3%)
  matrix products  1.94 us (2%)
  local copies, waits for them, and re-layouts  1.62 us (2%)
  between operations  0.83 us (1%)
    all_to_all x3, blocking collectives, exchange(): return lax.all_to_all(x, axis, 0, 0, axis_index_groups=[order])  39.8 us
    all_to_all x1, starting transfers between devices, exchange(): return lax.all_to_all(x, axis, 0, 0, axis_index_groups=[order])  14.1 us
    all_gather x1, blocking collectives, body(): pair = lax.all_gather(payload, 'core', axis=0)  8.46 us
    all_gather x1, blocking collectives, body(): lax.all_gather(full.reshape(half, dates, width), 'core', axis=0, tiled=True)  4.26 us
    all_gather x1, blocking collectives, body(): both = lax.all_gather(update, 'core', axis=0, tiled=True)  3.57 us
    all_to_all x1, waiting for transfers between devices, exchange(): return lax.all_to_all(x, axis, 0, 0, axis_index_groups=[order])  2.48 us
  transfers between devices with their start and end apart: 1, of which 1 were waited for; matrix products, arithmetic and copies ran while one was open for 4% of the time, Pallas kernels for 0%

profile of v8, /device:TPU:1, one launch (start us, length us, event | category | flops | bytes accessed | tf_op | source)
XLA Modules:
  0.0 81.7 jit_solution(18407686767148925602)
XLA Ops:
  0.6 0.0 copy-start
  0.6 1.2 %join.1 = (f32[120,256]{1,0:T(8,128)S(1)}, s32[8,128]{1,0:T(8,128)S(1)}) custom-call(s32[1,512]{1,0:T(1,128)} %bitcast.30, s32[1,256]{1,0:T(1,128)} %bitcast.32, f32[80,256]{1,0:T(8,128)} %refs_2_.1, f32[32,256]{1,0:T(8,128)} %refs_3_.1, s32[1,512]{1,0:T(1,128)} %bitcast.31), custom_call_target="tpu_custom_call" | custom-call | tf_op jit(solution)/shard_map/join/pallas_call | solution.py:241
  1.9 8.5 %all-gather = f32[240,256]{1,0:T(8,128)S(1)} all-gather(f32[120,256]{1,0:T(8,128)S(1)} %get-tuple-element.14), channel_id=2, replica_groups=mesh['chip'=64,'core'=2,'rhs'=4] {'core'}, dimensions={0}, use_global_device_ids=true | all-gather | bytes 368640 | tf_op jit(solution)/shard_map/all_gather | solution.py:260
  10.4 1.2 %pack.1 = f32[512,128]{1,0:T(8,128)} custom-call(f32[2,120,256]{2,1,0:T(8,128)S(1)} %bitcast.24), custom_call_target="tpu_custom_call" | custom-call | tf_op jit(solution)/shard_map/pack/pallas_call | solution.py:261
  11.5 0.0 copy-start.1
  11.5 14.1 %all-to-all-start = ((f32[64,8,128]{2,1,0:T(8,128)}), f32[64,8,128]{2,1,0:T(8,128)S(1)}, u32[]{:S(2)}, u32[]{:S(2)}) async-start(f32[64,8,128]{2,1,0:T(8,128)} %bitcast.28), calls=%async_computation | async-start | bytes 524288 | tf_op jit(solution)/shard_map/all_to_all | solution.py:25
  25.7 0.0 copy-done.1
  25.7 0.6 fusion.9
  26.3 0.0 copy-start.2
  26.3 0.1 fusion.4
  26.4 0.9 %copy-done.2 = f32[4,128,128]{2,1,0:T(8,128)S(1)} copy-done((f32[4,128,128]{2,1,0:T(8,128)S(1)}, f32[4,128,128]{2,1,0:T(8,128)}, u32[]{:S(2)}) %copy-start.2) | copy-done | bytes 262168
  27.3 0.6 reduce-precision_convert_fusion.2
  27.9 0.4 fusion.11
  28.4 0.0 copy-done
  28.4 0.3 reduce-precision_convert_fusion.3
  28.7 0.7 dynamic-slice_bitcast_fusion.rhs_ref
  29.5 0.1 fusion.3.both_ref
  29.5 2.5 %all-to-all-done = f32[64,8,128]{2,1,0:T(8,128)S(1)} async-done(((f32[64,8,128]{2,1,0:T(8,128)}), f32[64,8,128]{2,1,0:T(8,128)S(1)}, u32[]{:S(2)}, u32[]{:S(2)}) %all-to-all-start) | async-done | bytes 262176 | tf_op jit(solution)/shard_map/all_to_all | solution.py:25
  32.0 0.1 turn.1
  32.2 8.3 %all_to_all.20.refs_1_ = f32[4,32,512]{2,1,0:T(8,128)S(1)} all-to-all(f32[4,32,512]{2,1,0:T(8,128)S(1)} %get-tuple-element.17), channel_id=1, replica_groups={{2,3,0,1},{6,7,4,5},{10,11,8,9},{14,15,12,13},{18,19,16,17},{22,23,20,2..., dimensions={0} | all-to-all | bytes 524288 | tf_op jit(solution)/shard_map/all_to_all | solution.py:25
  40.4 0.7 forward.1
  41.1 3.6 %all_gather.14.both_ref = f32[8,80,128]{2,1,0:T(8,128)S(1)} all-gather(f32[4,80,128]{2,1,0:T(8,128)S(1)} %get-tuple-element.19), channel_id=1, replica_groups=mesh['chip'=64,'core'=2,'rhs'=4] {'core'}, dimensions={0}, use_global_device_ids=true | all-gather | bytes 491520 | tf_op jit(solution)/shard_map/all_gather | solution.py:300
  44.7 0.1 reduce.1
  44.8 16.2 %all_to_all.21 = f32[64,1,640]{2,1,0:T(1,128)S(1)} all-to-all(f32[64,1,640]{2,1,0:T(1,128)S(1)} %bitcast.27), channel_id=1, replica_groups={{288,296,304,312,256,264,272,280,352,360,368,376,320,328,336,344,416,42..., dimensions={0} | all-to-all | bytes 327680 | tf_op jit(solution)/shard_map/all_to_all | solution.py:25
  61.1 0.2 middle.1
  61.2 15.3 %all_to_all.22 = f32[64,1,640]{2,1,0:T(1,128)S(1)} all-to-all(f32[64,1,640]{2,1,0:T(1,128)S(1)} %bitcast.26), channel_id=1, replica_groups={{288,296,304,312,256,264,272,280,352,360,368,376,320,328,336,344,416,42..., dimensions={0} | all-to-all | bytes 327680 | tf_op jit(solution)/shard_map/all_to_all | solution.py:25
  76.5 4.3 %all_gather.15.top_ref = f32[8,80,128]{2,1,0:T(8,128)S(1)} all-gather(f32[4,80,128]{2,1,0:T(8,128)S(1)} %bitcast.29), channel_id=1, replica_groups=mesh['chip'=64,'core'=2,'rhs'=4] {'core'}, dimensions={0}, use_global_device_ids=true | all-gather | bytes 491520 | tf_op jit(solution)/shard_map/all_gather | solution.py:317
  80.8 1.0 %last.1 = (f32[4,80,128]{2,1,0:T(8,128)}, f32[8,80,128]{2,1,0:T(8,128)}) custom-call(s32[8,128]{1,0:T(8,128)S(1)} %get-tuple-element.13.parent_ref, f32[8,80,128]{2,1,0:T(8,128)S(1)} %all_gather.15.top_ref, bf16[320,384]{1,0:T(8,128)(2,1)S(1)} %get-tuple-element.22.rows_ref, bf16[4,768,128]{2,1,0:T(8,128)(2,1)S(1)} %fusion.3.both_ref), custom_call_target="tpu_custom_call" | custom-call | tf_op jit(solution)/shard_map/last/pallas_call | solution.py:318
  (4 shorter events, 0.1 us)
Async XLA Ops:
  0.6 27.7 %copy-start = (f32[8,128,128]{2,1,0:T(8,128)S(1)}, f32[8,128,128]{2,1,0:T(8,128)}, u32[]{:S(2)}) copy-start(f32[8,128,128]{2,1,0:T(8,128)} %param.16) | copy-start | bytes 1572868
  11.5 14.2 %copy-start.1 = (f32[4,128,128]{2,1,0:T(8,128)S(1)}, f32[4,128,128]{2,1,0:T(8,128)}, u32[]{:S(2)}) copy-start(f32[4,128,128]{2,1,0:T(8,128)} %param.14) | copy-start | bytes 786436
  11.5 20.5 %all-to-all-start = ((f32[64,8,128]{2,1,0:T(8,128)}), f32[64,8,128]{2,1,0:T(8,128)S(1)}, u32[]{:S(2)}, u32[]{:S(2)}) async-start(f32[64,8,128]{2,1,0:T(8,128)} %bitcast.28), calls=%async_computation | async-start | bytes 524288 | tf_op jit(solution)/shard_map/all_to_all | solution.py:25
  26.3 1.0 %copy-start.2 = (f32[4,128,128]{2,1,0:T(8,128)S(1)}, f32[4,128,128]{2,1,0:T(8,128)}, u32[]{:S(2)}) copy-start(f32[4,128,128]{2,1,0:T(8,128)} %param.15) | copy-start | bytes 786436

commit v9 on v7

--- a/solution.py
+++ b/solution.py
@@ -213,12 +213,14 @@
     top_ref,
     rows_ref,
     back_ref,
-    inv_ref,
-    off_ref,
+    inv_hbm,
+    off_hbm,
     out_hbm,
     top_hbm,
     out_ref,
     own_ref,
+    inv_ref,
+    off_ref,
     sems,
     *,
     chips,
@@ -243,6 +245,12 @@
 
     @pl.when(late)
     def _():
+        get_inv = pltpu.make_async_copy(inv_hbm, inv_ref, sems.at[1 + local])
+        get_off = pltpu.make_async_copy(off_hbm, off_ref, sems.at[2 + local])
+        get_inv.start()
+        get_off.start()
+        get_inv.wait()
+        get_off.wait()
         fill_back(inv_ref, off_ref, own_ref)
         solve(own_ref)
 
@@ -363,15 +371,17 @@
             jax.ShapeDtypeStruct((local, dates, width), F32),
             jax.ShapeDtypeStruct((tops, dates, width), F32),
         ),
-        in_specs=[VM] * 6,
+        in_specs=[VM, VM, VM, VM, ANY, ANY],
         out_specs=(ANY, ANY),
         scratch_shapes=[
             pltpu.VMEM((local, dates, width), F32),
             pltpu.VMEM((local, 6 * width, width), BF16),
-            pltpu.SemaphoreType.DMA((1 + local,)),
+            pltpu.VMEM((local, width, width), F32),
+            pltpu.VMEM((local, width, width), F32),
+            pltpu.SemaphoreType.DMA((3 + local,)),
         ],
         name="last",
-    )(*vmem(parent, full, parts, back_by, leaf_inv, leaf_off))
+    )(*vmem(parent, full, parts, back_by), leaf_inv, leaf_off)
 
 
 def solution(mesh):

time: 82.4 us -> 82.4 us (level)
  no operation moved by 1% of the time
where the time goes in v9:
time: 82.4 us; the launch traced here: 81.8 us
  blocking collectives  76.5 us (93%)
  Pallas kernels  4.65 us (6%)
    all_to_all x4, blocking collectives, exchange(): return lax.all_to_all(x, axis, 0, 0, axis_index_groups=[order])  60 us
    all_gather x1, blocking collectives, body(): pair = lax.all_gather(payload, 'core', axis=0)  8.46 us
    all_gather x1, blocking collectives, body(): lax.all_gather(full.reshape(half, dates, width), 'core', axis=0, tiled=True)  4.26 us
    all_gather x1, blocking collectives, body(): both = lax.all_gather(update, 'core', axis=0, tiled=True)  3.7 us
    pallas_call x1, Pallas kernels, body(): pl.pallas_call(lambda *refs: join_kernel(*refs, cores=cores), out_shape=(...  1.92 us

profile of v9, /device:TPU:1, one launch (start us, length us, event | category | flops | bytes accessed | tf_op | source)
XLA Modules:
  0.0 81.8 jit_solution(16773613682798565744)
XLA Ops:
  0.6 1.9 %join.1 = (f32[120,256]{1,0:T(8,128)S(1)}, s32[8,128]{1,0:T(8,128)S(1)}, bf16[4,128,384]{2,1,0:T(8,128)(2,1)S(1)}, bf16[4,768,128]{2,1,0:T(8,128)(2,1)S(1)}) custom-call(s32[1,512]{1,0:T(1,128)} %bitcast.17, s32[1,512]{1,0:T(1,128)} %bitcast.18, s32[1,256]{1,0:T(1,128)} %bitcast.19, f32[80,256]{1,0:T(8,128)} %refs_3_.1, f32[32,256]{1,0:T(8,128)} %refs_4_.2, ...), custom_call_target="tpu_custom_call" | custom-call | tf_op jit(solution)/shard_map/join/pallas_call | solution.py:297
  2.6 8.5 %all-gather = f32[240,256]{1,0:T(8,128)S(1)} all-gather(f32[120,256]{1,0:T(8,128)S(1)} %get-tuple-element.11), channel_id=2, replica_groups=mesh['chip'=64,'core'=2,'rhs'=4] {'core'}, dimensions={0}, use_global_device_ids=true | all-gather | bytes 368640 | tf_op jit(solution)/shard_map/all_gather | solution.py:325
  11.0 0.3 pack.1
  11.3 20.1 %all_to_all.20 = f32[64,8,128]{2,1,0:T(8,128)S(1)} all-to-all(f32[64,8,128]{2,1,0:T(8,128)S(1)} %bitcast.11), channel_id=1, replica_groups={{288,296,304,312,256,264,272,280,352,360,368,376,320,328,336,344,416,42..., dimensions={0} | all-to-all | bytes 524288 | tf_op jit(solution)/shard_map/all_to_all | solution.py:24
  31.5 0.1 turn.1
  31.6 8.3 %all_to_all.21.refs_1_ = f32[4,32,512]{2,1,0:T(8,128)S(1)} all-to-all(f32[4,32,512]{2,1,0:T(8,128)S(1)} %get-tuple-element.13), channel_id=1, replica_groups={{2,3,0,1},{6,7,4,5},{10,11,8,9},{14,15,12,13},{18,19,16,17},{22,23,20,2..., dimensions={0} | all-to-all | bytes 524288 | tf_op jit(solution)/shard_map/all_to_all | solution.py:24
  39.9 0.8 %forward.1 = (bf16[320,384]{1,0:T(8,128)(2,1)S(1)}, f32[4,80,128]{2,1,0:T(8,128)S(1)}) custom-call(f32[128,512]{1,0:T(8,128)S(1)} %get-tuple-element.12.refs_0_, f32[4,32,512]{2,1,0:T(8,128)S(1)} %all_to_all.21.refs_1_, bf16[4,128,384]{2,1,0:T(8,128)(2,1)S(1)} %get-tuple-element.14.refs_2_), custom_call_target="tpu_custom_call" | custom-call | tf_op jit(solution)/shard_map/forward/pallas_call | solution.py:343
  40.7 0.0 copy-start.1
  40.7 3.7 %all_gather.14.both_ref = f32[8,80,128]{2,1,0:T(8,128)S(1)} all-gather(f32[4,80,128]{2,1,0:T(8,128)S(1)} %get-tuple-element.15), channel_id=1, replica_groups=mesh['chip'=64,'core'=2,'rhs'=4] {'core'}, dimensions={0}, use_global_device_ids=true | all-gather | bytes 491520 | tf_op jit(solution)/shard_map/all_gather | solution.py:350
  44.4 0.0 copy-start
  44.4 0.1 reduce.1
  44.6 16.4 %all_to_all.22 = f32[64,1,640]{2,1,0:T(1,128)S(1)} all-to-all(f32[64,1,640]{2,1,0:T(1,128)S(1)} %bitcast.15), channel_id=1, replica_groups={{288,296,304,312,256,264,272,280,352,360,368,376,320,328,336,344,416,42..., dimensions={0} | all-to-all | bytes 327680 | tf_op jit(solution)/shard_map/all_to_all | solution.py:24
  60.9 0.0 copy-done.1
  60.9 0.0 copy-done
  60.9 0.3 middle.1
  61.3 15.3 %all_to_all.23 = f32[64,1,640]{2,1,0:T(1,128)S(1)} all-to-all(f32[64,1,640]{2,1,0:T(1,128)S(1)} %bitcast.14), channel_id=1, replica_groups={{288,296,304,312,256,264,272,280,352,360,368,376,320,328,336,344,416,42..., dimensions={0} | all-to-all | bytes 327680 | tf_op jit(solution)/shard_map/all_to_all | solution.py:24
  76.6 4.3 %all_gather.15.refs_1_ = f32[8,80,128]{2,1,0:T(8,128)S(1)} all-gather(f32[4,80,128]{2,1,0:T(8,128)S(1)} %bitcast.16), channel_id=1, replica_groups=mesh['chip'=64,'core'=2,'rhs'=4] {'core'}, dimensions={0}, use_global_device_ids=true | all-gather | bytes 491520 | tf_op jit(solution)/shard_map/all_gather | solution.py:367
  80.8 1.0 %last.1 = (f32[4,80,128]{2,1,0:T(8,128)}, f32[8,80,128]{2,1,0:T(8,128)}) custom-call(s32[8,128]{1,0:T(8,128)S(1)} %get-tuple-element.10.parent_ref.refs_0_, f32[8,80,128]{2,1,0:T(8,128)S(1)} %all_gather.15.refs_1_, bf16[320,384]{1,0:T(8,128)(2,1)S(1)} %get-tuple-element.16.refs_2_, bf16[4,768,128]{2,1,0:T(8,128)(2,1)S(1)} %get-tuple-element.17.refs_3_, ...), custom_call_target="tpu_custom_call" | custom-call | tf_op jit(solution)/shard_map/last/pallas_call | solution.py:368
Async XLA Ops:
  40.7 20.2 %copy-start.1 = (f32[8,80,128]{2,1,0:T(8,128)S(1)}, f32[8,80,128]{2,1,0:T(8,128)}, u32[]{:S(2)}) copy-start(f32[8,80,128]{2,1,0:T(8,128)} %refs_1_.1) | copy-start | bytes 983044
  44.4 16.5 %copy-start = (f32[8,128,128]{2,1,0:T(8,128)S(1)}, f32[8,128,128]{2,1,0:T(8,128)}, u32[]{:S(2)}) copy-start(f32[8,128,128]{2,1,0:T(8,128)} %refs_2_.1) | copy-start | bytes 1572868

commit v10 on v6

--- a/solution.py
+++ b/solution.py
@@ -16,7 +16,7 @@
 
 def far_index(count):
     side = math.isqrt(count)
-    return side // 2 * side + side // 2
+    return side // 2 * side + side // 2 + 1
 
 
 def exchange(x, axis, far):

time: 81.9 us -> 81.9 us (level)
  no operation moved by 1% of the time
where the time goes in v10:
time: 81.9 us; the launch traced here: 81.6 us
  blocking collectives  76.5 us (93%)
  Pallas kernels  4.45 us (5%)
    all_to_all x4, blocking collectives, exchange(): return lax.all_to_all(x, axis, 0, 0, axis_index_groups=[order])  59.6 us
    all_gather x1, blocking collectives, body(): pair = lax.all_gather(payload, 'core', axis=0)  8.46 us
    all_gather x1, blocking collectives, body(): lax.all_gather(full.reshape(half, dates, width), 'core', axis=0, tiled=True)  4.24 us
    all_gather x1, blocking collectives, body(): both = lax.all_gather(update, 'core', axis=0, tiled=True)  4.22 us

profile of v10, /device:TPU:1, one launch (start us, length us, event | category | flops | bytes accessed | tf_op | source)
XLA Modules:
  0.0 81.6 jit_solution(12117561741035931551)
XLA Ops:
  0.6 1.5 %join.1 = (f32[120,256]{1,0:T(8,128)S(1)}, s32[8,128]{1,0:T(8,128)S(1)}, bf16[4,256,384]{2,1,0:T(8,128)(2,1)S(1)}, bf16[4,768,128]{2,1,0:T(8,128)(2,1)S(1)}) custom-call(s32[1,512]{1,0:T(1,128)} %bitcast.17, s32[1,512]{1,0:T(1,128)} %bitcast.18, s32[1,256]{1,0:T(1,128)} %bitcast.19, f32[80,256]{1,0:T(8,128)} %refs_3_.1, f32[32,256]{1,0:T(8,128)} %refs_4_.1, ...), custom_call_target="tpu_custom_call" | custom-call | tf_op jit(solution)/shard_map/join/pallas_call | solution.py:251
  2.1 8.5 %all-gather = f32[240,256]{1,0:T(8,128)S(1)} all-gather(f32[120,256]{1,0:T(8,128)S(1)} %get-tuple-element.11), channel_id=2, replica_groups=mesh['chip'=64,'core'=2,'rhs'=4] {'core'}, dimensions={0}, use_global_device_ids=true | all-gather | bytes 368640 | tf_op jit(solution)/shard_map/all_gather | solution.py:279
  10.6 0.3 pack.1
  10.9 19.7 %all_to_all.20 = f32[64,8,128]{2,1,0:T(8,128)S(1)} all-to-all(f32[64,8,128]{2,1,0:T(8,128)S(1)} %bitcast.11), channel_id=1, replica_groups={{296,288,312,304,264,256,280,272,360,352,376,368,328,320,344,336,424,41..., dimensions={0} | all-to-all | bytes 524288 | tf_op jit(solution)/shard_map/all_to_all | solution.py:24
  30.6 0.1 turn.1
  30.8 8.0 %all_to_all.21.refs_1_ = f32[4,32,512]{2,1,0:T(8,128)S(1)} all-to-all(f32[4,32,512]{2,1,0:T(8,128)S(1)} %get-tuple-element.13), channel_id=1, replica_groups={{2,3,0,1},{6,7,4,5},{10,11,8,9},{14,15,12,13},{18,19,16,17},{22,23,20,2..., dimensions={0} | all-to-all | bytes 524288 | tf_op jit(solution)/shard_map/all_to_all | solution.py:24
  38.8 1.1 %forward.1 = (bf16[320,384]{1,0:T(8,128)(2,1)S(1)}, f32[4,80,128]{2,1,0:T(8,128)S(1)}) custom-call(f32[128,512]{1,0:T(8,128)S(1)} %get-tuple-element.12.refs_0_, f32[4,32,512]{2,1,0:T(8,128)S(1)} %all_to_all.21.refs_1_, bf16[4,256,384]{2,1,0:T(8,128)(2,1)S(1)} %get-tuple-element.14.refs_2_), custom_call_target="tpu_custom_call" | custom-call | tf_op jit(solution)/shard_map/forward/pallas_call | solution.py:297
  39.8 0.0 copy-start.1
  39.8 4.2 %all_gather.14.both_ref = f32[8,80,128]{2,1,0:T(8,128)S(1)} all-gather(f32[4,80,128]{2,1,0:T(8,128)S(1)} %get-tuple-element.15), channel_id=1, replica_groups=mesh['chip'=64,'core'=2,'rhs'=4] {'core'}, dimensions={0}, use_global_device_ids=true | all-gather | bytes 491520 | tf_op jit(solution)/shard_map/all_gather | solution.py:304
  44.1 0.0 copy-start
  44.1 0.1 reduce.1
  44.2 16.4 %all_to_all.22 = f32[64,1,640]{2,1,0:T(1,128)S(1)} all-to-all(f32[64,1,640]{2,1,0:T(1,128)S(1)} %bitcast.15), channel_id=1, replica_groups={{296,288,312,304,264,256,280,272,360,352,376,368,328,320,344,336,424,41..., dimensions={0} | all-to-all | bytes 327680 | tf_op jit(solution)/shard_map/all_to_all | solution.py:24
  60.6 0.0 copy-done.1
  60.6 0.0 copy-done
  60.6 0.3 middle.1
  60.9 15.4 %all_to_all.23 = f32[64,1,640]{2,1,0:T(1,128)S(1)} all-to-all(f32[64,1,640]{2,1,0:T(1,128)S(1)} %bitcast.14), channel_id=1, replica_groups={{296,288,312,304,264,256,280,272,360,352,376,368,328,320,344,336,424,41..., dimensions={0} | all-to-all | bytes 327680 | tf_op jit(solution)/shard_map/all_to_all | solution.py:24
  76.4 4.2 %all_gather.15.top_ref = f32[8,80,128]{2,1,0:T(8,128)S(1)} all-gather(f32[4,80,128]{2,1,0:T(8,128)S(1)} %bitcast.16), channel_id=1, replica_groups=mesh['chip'=64,'core'=2,'rhs'=4] {'core'}, dimensions={0}, use_global_device_ids=true | all-gather | bytes 491520 | tf_op jit(solution)/shard_map/all_gather | solution.py:321
  80.6 1.0 %last.1 = (f32[4,80,128]{2,1,0:T(8,128)}, f32[8,80,128]{2,1,0:T(8,128)}) custom-call(s32[8,128]{1,0:T(8,128)S(1)} %get-tuple-element.10.parent_ref, f32[8,80,128]{2,1,0:T(8,128)S(1)} %all_gather.15.top_ref, bf16[320,384]{1,0:T(8,128)(2,1)S(1)} %get-tuple-element.16.rows_ref, bf16[4,768,128]{2,1,0:T(8,128)(2,1)S(1)} %get-tuple-element.17.by_ref), custom_call_target="tpu_custom_call" | custom-call | tf_op jit(solution)/shard_map/last/pallas_call | solution.py:322
Async XLA Ops:
  39.8 20.8 %copy-start.1 = (f32[8,80,128]{2,1,0:T(8,128)S(1)}, f32[8,80,128]{2,1,0:T(8,128)}, u32[]{:S(2)}) copy-start(f32[8,80,128]{2,1,0:T(8,128)} %refs_1_.1) | copy-start | bytes 983044
  44.1 16.5 %copy-start = (f32[8,128,128]{2,1,0:T(8,128)S(1)}, f32[8,128,128]{2,1,0:T(8,128)}, u32[]{:S(2)}) copy-start(f32[8,128,128]{2,1,0:T(8,128)} %refs_2_.1) | copy-start | bytes 1572868
